TPU v7x, 32 devices: a whole 2x2x4 slice. The times are simulated.
32 devices in a mesh: field: 2 (over x), tm: 4 (over y, core), tile: 4 (over z).
Axes of the slice: x: 2, y: 2, z: 4, core: 2. Of those that a mesh axis runs over, the one named last changes fastest.
Arguments:
- movie: bfloat16 [32, 1024, 1024], P(('field', 'tm'), 'tile'), parts along dimension 0, may hold values from -6 to 6
- patch_in: bfloat16 [16, 64], replicated, may hold values from -1.5 to 1.5
- patch_bias: float32 [64], replicated, may hold values from -3 to 3
- conv_weight: bfloat16 [2, 9, 64, 64], replicated, may hold values from -0.25 to 0.25
- conv_bias: float32 [2, 64], replicated, may hold values from -3 to 3
- patch_out: bfloat16 [64, 16], replicated, may hold values from -0.75 to 0.75
- footprint: bfloat16 [128, 64, 1024], P(('field', 'tile'), 'tm'), parts along dimension 0, may hold values from 0 to 0.0625
- slot_cell: int32 [128, 64], P(('field', 'tile')), parts along dimension 0, may hold values from 0 to 3071, as said below
- slot_window_index: int32 [128, 64], P(('field', 'tile')), parts along dimension 0, may hold values from 0 to 15
- decay: float32 [6144], P(('field', 'tm', 'tile')), parts along dimension 0, may hold values from 0.3 to 0.95
Outputs:
- activity: float32 [16, 6144], P(None, ('field', 'tm', 'tile')), parts along dimension 1
There are 2 independent parts, one for each index of `field`. A program takes and returns all parts, laid end to end along the dimension named above; an argument that names none is the same for every part. Nothing has to cross between parts.
Inputs may be any that keep to these rules, and one draw needn't show every extreme that they name: `slot_cell`: every one of the 3072 cells is named by at least one slot.
All inputs are finite; a program needn't handle non-finite values.
Results may differ from a plain program's by a relative error of at most 0.0069.
Values may be sent and summed in bfloat16 or wider, within the bound.
No kernel may reach another device: no remote copies, remote signals or barrier semaphores. Data moves between devices by JAX's collectives and lax.ppermute only.
A program may use at most 192 MiB of HBM per device.

v0:
```python
import jax
import jax.numpy as jnp
from jax import lax
from jax.sharding import PartitionSpec as P

BLK = 128


def with_halo(block, sides, width):
    for axis, dim in sides:
        count = lax.axis_size(axis)
        forward = [(i, i + 1) for i in range(count - 1)]
        backward = [(target, source) for source, target in forward]
        low = lax.ppermute(
            lax.slice_in_dim(block, block.shape[dim] - width, None, axis=dim), axis, forward
        )
        high = lax.ppermute(lax.slice_in_dim(block, 0, width, axis=dim), axis, backward)
        block = jnp.concatenate([low, block, high], axis=dim)
    return block


def conv_rows(extended, weights, bias, rows_out):
    channels = extended.shape[3]
    stacked_weights = (
        weights.reshape(3, 3, channels, channels)
        .transpose(0, 3, 1, 2)
        .reshape(3, channels, 3 * channels)
    )

    def single(frame):
        width = frame.shape[1]
        taps = jnp.einsum(
            "rwc,cn->rwn", frame[0:rows_out], stacked_weights[0], preferred_element_type=jnp.float32
        )
        taps = taps + jnp.einsum(
            "rwc,cn->rwn",
            frame[1 : 1 + rows_out],
            stacked_weights[1],
            preferred_element_type=jnp.float32,
        )
        taps = taps + jnp.einsum(
            "rwc,cn->rwn",
            frame[2 : 2 + rows_out],
            stacked_weights[2],
            preferred_element_type=jnp.float32,
        )
        blank = jnp.zeros((rows_out, 1, channels), jnp.float32)
        summed = taps[:, :, channels : 2 * channels]
        summed = summed + jnp.concatenate([blank, taps[:, 0 : width - 1, 0:channels]], axis=1)
        summed = summed + jnp.concatenate(
            [taps[:, 1:width, 2 * channels : 3 * channels], blank], axis=1
        )
        center = frame[1 : 1 + rows_out].astype(jnp.float32)
        return (center + jax.nn.relu(summed + bias[None, None, :])).astype(jnp.bfloat16)

    return lax.map(single, extended)


def slot_matrix(owners, cell_count):
    labels = jnp.arange(cell_count, dtype=jnp.int32)
    return (owners[:, None] == labels[None, :]).astype(jnp.float32)


def body(
    movie,
    patch_in,
    patch_bias,
    conv_weight,
    conv_bias,
    patch_out,
    footprint,
    slot_cell,
    slot_window_index,
    decay,
):
    frame_count, tile_rows, image_width = movie.shape
    coarse_rows = tile_rows // 4
    coarse_cols = image_width // 4
    layers = conv_weight.shape[0]
    raw = movie.reshape(frame_count, coarse_rows, 4, coarse_cols, 4).transpose(0, 1, 3, 2, 4)
    raw = raw.reshape(frame_count, coarse_rows, coarse_cols, 16)

    def embed(frame_raw):
        summed = jnp.einsum("ruk,kc->ruc", frame_raw, patch_in, preferred_element_type=jnp.float32)
        return jax.nn.relu(summed + patch_bias[None, None, :]).astype(jnp.bfloat16)

    features = lax.map(embed, raw)
    for layer in range(layers):
        extended = with_halo(features, (("tile", 1),), 1)
        features = conv_rows(extended, conv_weight[layer], conv_bias[layer], coarse_rows)

    def decode(pair):
        frame_features, frame_raw = pair
        summed = jnp.einsum(
            "ruc,ck->ruk", frame_features, patch_out, preferred_element_type=jnp.float32
        )
        return (summed + frame_raw.astype(jnp.float32)).astype(jnp.bfloat16)

    decoded = lax.map(decode, (features, raw))
    denoised = decoded.reshape(frame_count, coarse_rows, coarse_cols, 4, 4).transpose(0, 1, 3, 2, 4)
    denoised = denoised.reshape(frame_count, tile_rows, image_width)
    block_rows = tile_rows // BLK
    block_cols = image_width // BLK
    win = BLK // 4
    windows = denoised.reshape(frame_count, block_rows, 4, win, block_cols, 4, win)
    windows = windows.transpose(0, 1, 4, 2, 5, 3, 6).reshape(
        frame_count, block_rows * block_cols, 16, win * win
    )
    selector = (
        slot_window_index[:, :, None] == jnp.arange(16, dtype=jnp.int32)[None, None, :]
    ).astype(jnp.float32)
    own_cells = decay.shape[0]
    cell_count = own_cells * lax.axis_size("tm") * lax.axis_size("tile")
    every = jnp.einsum(
        "bsp,fbqp->fbsq",
        lax.all_gather(footprint, "tm", axis=1, tiled=True),
        windows,
        preferred_element_type=jnp.float32,
    )
    slot_sums = jnp.sum(every * selector[None], axis=3)
    onehot = slot_matrix(slot_cell.reshape(-1), cell_count)
    per_cell = jnp.dot(slot_sums.reshape(frame_count, -1), onehot, precision=lax.Precision.HIGHEST)
    grouped = per_cell.reshape(frame_count, lax.axis_size("tm"), lax.axis_size("tile"), own_cells)
    reduced = lax.psum_scatter(grouped, "tile", scatter_dimension=2, tiled=True)
    moved = lax.all_to_all(reduced, "tm", split_axis=1, concat_axis=0, tiled=True)
    traces = moved.reshape(-1, own_cells)
    centered = traces - jnp.mean(traces, axis=0)[None, :]
    previous = jnp.concatenate([jnp.zeros((1, own_cells), jnp.float32), centered[:-1]], axis=0)
    spikes = centered - decay[None, :] * previous
    scale = jnp.sqrt(jnp.mean(spikes * spikes, axis=0) + 1e-05)
    return spikes / scale[None, :]


def solution(mesh):
    placed = (
        P(("field", "tm"), "tile", None),
        P(),
        P(),
        P(),
        P(),
        P(),
        P(("field", "tile"), "tm", None),
        P(("field", "tile"), None),
        P(("field", "tile"), None),
        P(("field", "tm", "tile")),
    )
    return jax.shard_map(
        body,
        mesh=mesh,
        in_specs=placed,
        out_specs=P(None, ("field", "tm", "tile")),
        check_vma=False,
    )
```

profile of v0, /device:TPU:0, one launch (start us, length us, event | category | flops | bytes accessed | tf_op | source)
XLA Modules:
  0.0 772.7 jit_solution(2185316189194329004)
XLA Ops:
  6.5 145.9 %reshape.74 = bf16[4,64,4,256,4]{4,3,2,1,0:T(8,128)(2,1)} reshape(bf16[4,256,1024]{2,1,0:T(8,128)(2,1)} %param.18) | data formatting | bytes 4194304 | tf_op jit(solution)/shard_map/reshape | solution.py:80
  152.5 55.9 %copy.33 = bf16[4,64,256,4,4]{2,1,4,3,0:T(8,128)(2,1)} copy(bf16[4,64,256,4,4]{4,2,3,1,0:T(8,128)(2,1)} %bitcast.29) | data formatting | bytes 4194304 | tf_op jit(solution)/shard_map/transpose | solution.py:80
  215.5 8.7 %while.40 = (s32[]{:T(128)}, bf16[4,64,256,64]{2,3,1,0:T(8,128)(2,1)}, bf16[4,64,256,16]{2,3,1,0:T(8,128)(2,1)S(1)}, bf16[16,64]{1,0:T(8,128)(2,1)S(1)}, f32[64]{0:T(128)S(1)}, /*index=5*/s32[]{:T(128)}) while((s32[]{:T(128)}, bf16[4,64,256,64]{2,3,1,0:T(8,128)(2,1)}, bf16[4,64,256,16]{2,3,1,0:T(8,128)(2,1)S(1)}, ...), condition=%wide.region_1.2_spmd, body=%wide.region_0.1_spmd.sunk | while | flops 36700160 | bytes 2627141 | solution.py:87
  249.2 153.9 %while.41 = (s32[]{:T(128)}, bf16[4,64,256,64]{2,3,1,0:T(8,128)(2,1)}, bf16[4,66,256,64]{2,3,1,0:T(8,128)(2,1)}, bf16[3,64,192]{2,1,0:T(8,128)(2,1)S(1)}, f32[1,...) while((s32[]{:T(128)}, bf16[4,64,256,64]{2,3,1,0:T(8,128)(2,1)}, ...), condition=%wide.region_3.4_spmd, body=%wide.region_2.3_spmd.sunk | while | flops 1221591040 | bytes 102795648 | solution.py:56
  249.3 8.0 %fusion.106 = f32[64,256,192]{1,2,0:T(8,128)} fusion(bf16[4,66,256,64]{2,3,1,0:T(8,128)(2,1)} %get-tuple-element.409, s32[]{:T(128)} %get-tuple-element.398, s32[]{:T(128)S(6)} %add.260, bf16[3,64,192]{2,1,0:T(8,128)(2,1)S(1)} %get-tuple-element.410), kind=kOutput, calls=%fused_computation.19.clone.1 | convolution fusion | flops 402653184 | bytes 14713348 | tf_op jit(solution)/shard_map/while/body/eval_jaxpr/rwc,cn->rwn/dot_general | solution.py:35
  257.2 8.0 %fusion.105 = f32[64,256,192]{1,2,0:T(8,128)} fusion(bf16[4,66,256,64]{2,3,1,0:T(8,128)(2,1)} %get-tuple-element.409, s32[]{:T(128)} %get-tuple-element.398, bf16[3,64,192]{2,1,0:T(8,128)(2,1)S(1)} %get-tuple-element.410), kind=kOutput, calls=%fused_computation.17.clone.1 | convolution fusion | flops 402653184 | bytes 14713344 | tf_op jit(solution)/shard_map/while/body/eval_jaxpr/rwc,cn->rwn/dot_general | solution.py:32
  265.2 10.7 %add_add_fusion.4 = f32[64,256,192]{1,2,0:T(8,128)S(1)} fusion(f32[64,256,192]{1,2,0:T(8,128)} %fusion.105, f32[64,256,192]{1,2,0:T(8,128)} %fusion.106, bf16[4,66,256,64]{2,3,1,0:T(8,128)(2,1)} %get-tuple-element.409, s32[]{:T(128)} %get-tuple-element.398, s32[]{:T(128)S(6)} %add.261, bf16[3,64,192]{2,1,0:T(8,128)(2,1)S(1)} %get-tuple-element.410), kind=kOutput, calls=%fused_computation.6.clone.1 | convolution fusion | flops 408944640 | bytes 39879172 | tf_op jit(solution)/shard_map/while/body/eval_jaxpr/rwc,cn->rwn/dot_general | solution.py:41
  287.8 7.9 %fusion.106 = f32[64,256,192]{1,2,0:T(8,128)} fusion(bf16[4,66,256,64]{2,3,1,0:T(8,128)(2,1)} %get-tuple-element.409, s32[]{:T(128)} %get-tuple-element.398, s32[]{:T(128)S(6)} %add.260, bf16[3,64,192]{2,1,0:T(8,128)(2,1)S(1)} %get-tuple-element.410), kind=kOutput, calls=%fused_computation.19.clone.1 | convolution fusion | flops 402653184 | bytes 14713348 | tf_op jit(solution)/shard_map/while/body/eval_jaxpr/rwc,cn->rwn/dot_general | solution.py:35
  295.7 8.0 %fusion.105 = f32[64,256,192]{1,2,0:T(8,128)} fusion(bf16[4,66,256,64]{2,3,1,0:T(8,128)(2,1)} %get-tuple-element.409, s32[]{:T(128)} %get-tuple-element.398, bf16[3,64,192]{2,1,0:T(8,128)(2,1)S(1)} %get-tuple-element.410), kind=kOutput, calls=%fused_computation.17.clone.1 | convolution fusion | flops 402653184 | bytes 14713344 | tf_op jit(solution)/shard_map/while/body/eval_jaxpr/rwc,cn->rwn/dot_general | solution.py:32
  303.6 10.7 %add_add_fusion.4 = f32[64,256,192]{1,2,0:T(8,128)S(1)} fusion(f32[64,256,192]{1,2,0:T(8,128)} %fusion.105, f32[64,256,192]{1,2,0:T(8,128)} %fusion.106, bf16[4,66,256,64]{2,3,1,0:T(8,128)(2,1)} %get-tuple-element.409, s32[]{:T(128)} %get-tuple-element.398, s32[]{:T(128)S(6)} %add.261, bf16[3,64,192]{2,1,0:T(8,128)(2,1)S(1)} %get-tuple-element.410), kind=kOutput, calls=%fused_computation.6.clone.1 | convolution fusion | flops 408944640 | bytes 39879172 | tf_op jit(solution)/shard_map/while/body/eval_jaxpr/rwc,cn->rwn/dot_general | solution.py:41
  334.1 8.0 %fusion.105 = f32[64,256,192]{1,2,0:T(8,128)} fusion(bf16[4,66,256,64]{2,3,1,0:T(8,128)(2,1)} %get-tuple-element.409, s32[]{:T(128)} %get-tuple-element.398, bf16[3,64,192]{2,1,0:T(8,128)(2,1)S(1)} %get-tuple-element.410), kind=kOutput, calls=%fused_computation.17.clone.1 | convolution fusion | flops 402653184 | bytes 14713344 | tf_op jit(solution)/shard_map/while/body/eval_jaxpr/rwc,cn->rwn/dot_general | solution.py:32
  342.1 10.7 %add_add_fusion.4 = f32[64,256,192]{1,2,0:T(8,128)S(1)} fusion(f32[64,256,192]{1,2,0:T(8,128)} %fusion.105, f32[64,256,192]{1,2,0:T(8,128)} %fusion.106, bf16[4,66,256,64]{2,3,1,0:T(8,128)(2,1)} %get-tuple-element.409, s32[]{:T(128)} %get-tuple-element.398, s32[]{:T(128)S(6)} %add.261, bf16[3,64,192]{2,1,0:T(8,128)(2,1)S(1)} %get-tuple-element.410), kind=kOutput, calls=%fused_computation.6.clone.1 | convolution fusion | flops 408944640 | bytes 39879172 | tf_op jit(solution)/shard_map/while/body/eval_jaxpr/rwc,cn->rwn/dot_general | solution.py:41
  364.7 7.9 %fusion.106 = f32[64,256,192]{1,2,0:T(8,128)} fusion(bf16[4,66,256,64]{2,3,1,0:T(8,128)(2,1)} %get-tuple-element.409, s32[]{:T(128)} %get-tuple-element.398, s32[]{:T(128)S(6)} %add.260, bf16[3,64,192]{2,1,0:T(8,128)(2,1)S(1)} %get-tuple-element.410), kind=kOutput, calls=%fused_computation.19.clone.1 | convolution fusion | flops 402653184 | bytes 14713348 | tf_op jit(solution)/shard_map/while/body/eval_jaxpr/rwc,cn->rwn/dot_general | solution.py:35
  372.6 8.0 %fusion.105 = f32[64,256,192]{1,2,0:T(8,128)} fusion(bf16[4,66,256,64]{2,3,1,0:T(8,128)(2,1)} %get-tuple-element.409, s32[]{:T(128)} %get-tuple-element.398, bf16[3,64,192]{2,1,0:T(8,128)(2,1)S(1)} %get-tuple-element.410), kind=kOutput, calls=%fused_computation.17.clone.1 | convolution fusion | flops 402653184 | bytes 14713344 | tf_op jit(solution)/shard_map/while/body/eval_jaxpr/rwc,cn->rwn/dot_general | solution.py:32
  380.5 10.7 %add_add_fusion.4 = f32[64,256,192]{1,2,0:T(8,128)S(1)} fusion(f32[64,256,192]{1,2,0:T(8,128)} %fusion.105, f32[64,256,192]{1,2,0:T(8,128)} %fusion.106, bf16[4,66,256,64]{2,3,1,0:T(8,128)(2,1)} %get-tuple-element.409, s32[]{:T(128)} %get-tuple-element.398, s32[]{:T(128)S(6)} %add.261, bf16[3,64,192]{2,1,0:T(8,128)(2,1)S(1)} %get-tuple-element.410), kind=kOutput, calls=%fused_computation.6.clone.1 | convolution fusion | flops 408944640 | bytes 39879172 | tf_op jit(solution)/shard_map/while/body/eval_jaxpr/rwc,cn->rwn/dot_general | solution.py:41
  426.1 153.9 %while.42 = (s32[]{:T(128)}, bf16[4,64,256,64]{2,3,1,0:T(8,128)(2,1)}, bf16[4,66,256,64]{2,3,1,0:T(8,128)(2,1)}, bf16[3,64,192]{2,1,0:T(8,128)(2,1)S(1)}, f32[1,...) while((s32[]{:T(128)}, bf16[4,64,256,64]{2,3,1,0:T(8,128)(2,1)}, ...), condition=%wide.region_5.6_spmd, body=%wide.region_4.5_spmd.sunk | while | flops 1221591040 | bytes 102795648 | solution.py:56
  426.1 7.9 %fusion.113 = f32[64,256,192]{1,2,0:T(8,128)} fusion(bf16[4,66,256,64]{2,3,1,0:T(8,128)(2,1)} %get-tuple-element.436, s32[]{:T(128)} %get-tuple-element.425, s32[]{:T(128)S(6)} %add.270, bf16[3,64,192]{2,1,0:T(8,128)(2,1)S(1)} %get-tuple-element.437), kind=kOutput, calls=%fused_computation.42.clone.1 | convolution fusion | flops 402653184 | bytes 14713348 | tf_op jit(solution)/shard_map/while/body/eval_jaxpr/rwc,cn->rwn/dot_general | solution.py:35
  434.0 8.0 %fusion.112 = f32[64,256,192]{1,2,0:T(8,128)} fusion(bf16[4,66,256,64]{2,3,1,0:T(8,128)(2,1)} %get-tuple-element.436, s32[]{:T(128)} %get-tuple-element.425, bf16[3,64,192]{2,1,0:T(8,128)(2,1)S(1)} %get-tuple-element.437), kind=kOutput, calls=%fused_computation.40.clone.1 | convolution fusion | flops 402653184 | bytes 14713344 | tf_op jit(solution)/shard_map/while/body/eval_jaxpr/rwc,cn->rwn/dot_general | solution.py:32
  442.0 10.7 %add_add_fusion.5 = f32[64,256,192]{1,2,0:T(8,128)S(1)} fusion(f32[64,256,192]{1,2,0:T(8,128)} %fusion.112, f32[64,256,192]{1,2,0:T(8,128)} %fusion.113, bf16[4,66,256,64]{2,3,1,0:T(8,128)(2,1)} %get-tuple-element.436, s32[]{:T(128)} %get-tuple-element.425, s32[]{:T(128)S(6)} %add.271, bf16[3,64,192]{2,1,0:T(8,128)(2,1)S(1)} %get-tuple-element.437), kind=kOutput, calls=%fused_computation.29.clone.1 | convolution fusion | flops 408944640 | bytes 39879172 | tf_op jit(solution)/shard_map/while/body/eval_jaxpr/rwc,cn->rwn/dot_general | solution.py:41
  472.5 8.0 %fusion.112 = f32[64,256,192]{1,2,0:T(8,128)} fusion(bf16[4,66,256,64]{2,3,1,0:T(8,128)(2,1)} %get-tuple-element.436, s32[]{:T(128)} %get-tuple-element.425, bf16[3,64,192]{2,1,0:T(8,128)(2,1)S(1)} %get-tuple-element.437), kind=kOutput, calls=%fused_computation.40.clone.1 | convolution fusion | flops 402653184 | bytes 14713344 | tf_op jit(solution)/shard_map/while/body/eval_jaxpr/rwc,cn->rwn/dot_general | solution.py:32
  480.4 10.7 %add_add_fusion.5 = f32[64,256,192]{1,2,0:T(8,128)S(1)} fusion(f32[64,256,192]{1,2,0:T(8,128)} %fusion.112, f32[64,256,192]{1,2,0:T(8,128)} %fusion.113, bf16[4,66,256,64]{2,3,1,0:T(8,128)(2,1)} %get-tuple-element.436, s32[]{:T(128)} %get-tuple-element.425, s32[]{:T(128)S(6)} %add.271, bf16[3,64,192]{2,1,0:T(8,128)(2,1)S(1)} %get-tuple-element.437), kind=kOutput, calls=%fused_computation.29.clone.1 | convolution fusion | flops 408944640 | bytes 39879172 | tf_op jit(solution)/shard_map/while/body/eval_jaxpr/rwc,cn->rwn/dot_general | solution.py:41
  503.1 7.9 %fusion.113 = f32[64,256,192]{1,2,0:T(8,128)} fusion(bf16[4,66,256,64]{2,3,1,0:T(8,128)(2,1)} %get-tuple-element.436, s32[]{:T(128)} %get-tuple-element.425, s32[]{:T(128)S(6)} %add.270, bf16[3,64,192]{2,1,0:T(8,128)(2,1)S(1)} %get-tuple-element.437), kind=kOutput, calls=%fused_computation.42.clone.1 | convolution fusion | flops 402653184 | bytes 14713348 | tf_op jit(solution)/shard_map/while/body/eval_jaxpr/rwc,cn->rwn/dot_general | solution.py:35
  511.0 8.0 %fusion.112 = f32[64,256,192]{1,2,0:T(8,128)} fusion(bf16[4,66,256,64]{2,3,1,0:T(8,128)(2,1)} %get-tuple-element.436, s32[]{:T(128)} %get-tuple-element.425, bf16[3,64,192]{2,1,0:T(8,128)(2,1)S(1)} %get-tuple-element.437), kind=kOutput, calls=%fused_computation.40.clone.1 | convolution fusion | flops 402653184 | bytes 14713344 | tf_op jit(solution)/shard_map/while/body/eval_jaxpr/rwc,cn->rwn/dot_general | solution.py:32
  518.9 10.7 %add_add_fusion.5 = f32[64,256,192]{1,2,0:T(8,128)S(1)} fusion(f32[64,256,192]{1,2,0:T(8,128)} %fusion.112, f32[64,256,192]{1,2,0:T(8,128)} %fusion.113, bf16[4,66,256,64]{2,3,1,0:T(8,128)(2,1)} %get-tuple-element.436, s32[]{:T(128)} %get-tuple-element.425, s32[]{:T(128)S(6)} %add.271, bf16[3,64,192]{2,1,0:T(8,128)(2,1)S(1)} %get-tuple-element.437), kind=kOutput, calls=%fused_computation.29.clone.1 | convolution fusion | flops 408944640 | bytes 39879172 | tf_op jit(solution)/shard_map/while/body/eval_jaxpr/rwc,cn->rwn/dot_general | solution.py:41
  549.4 8.0 %fusion.112 = f32[64,256,192]{1,2,0:T(8,128)} fusion(bf16[4,66,256,64]{2,3,1,0:T(8,128)(2,1)} %get-tuple-element.436, s32[]{:T(128)} %get-tuple-element.425, bf16[3,64,192]{2,1,0:T(8,128)(2,1)S(1)} %get-tuple-element.437), kind=kOutput, calls=%fused_computation.40.clone.1 | convolution fusion | flops 402653184 | bytes 14713344 | tf_op jit(solution)/shard_map/while/body/eval_jaxpr/rwc,cn->rwn/dot_general | solution.py:32
  557.3 10.7 %add_add_fusion.5 = f32[64,256,192]{1,2,0:T(8,128)S(1)} fusion(f32[64,256,192]{1,2,0:T(8,128)} %fusion.112, f32[64,256,192]{1,2,0:T(8,128)} %fusion.113, bf16[4,66,256,64]{2,3,1,0:T(8,128)(2,1)} %get-tuple-element.436, s32[]{:T(128)} %get-tuple-element.425, s32[]{:T(128)S(6)} %add.271, bf16[3,64,192]{2,1,0:T(8,128)(2,1)S(1)} %get-tuple-element.437), kind=kOutput, calls=%fused_computation.29.clone.1 | convolution fusion | flops 408944640 | bytes 39879172 | tf_op jit(solution)/shard_map/while/body/eval_jaxpr/rwc,cn->rwn/dot_general | solution.py:41
  580.0 11.5 %while.43 = (s32[]{:T(128)}, bf16[4,64,256,16]{2,3,1,0:T(8,128)(2,1)}, bf16[4,64,256,64]{2,3,1,0:T(8,128)(2,1)}, bf16[64,16]{0,1:T(8,128)(2,1)S(1)}, bf16[4,64,256,16]{2,3,1,0:T(8,128)(2,1)}, /*index=5*/s32[]{:T(128)}) while((s32[]{:T(128)}, bf16[4,64,256,16]{2,3,1,0:T(8,128)(2,1)}, bf16[4,64,256,64]{2,3,1,0:T(8,128)(2,1)}, ...), condition=%wide.region_7.8_spmd, body=%wide.region_6.7_spmd.sunk | while | flops 34340864 | bytes 3148869 | solution.py:99
  594.0 41.2 %copy.38 = bf16[4,64,256,4,4]{4,2,3,1,0:T(8,128)(2,1)} copy(bf16[4,64,256,4,4]{2,4,3,1,0:T(4,128)(2,1)S(1)} %reshape.78) | data formatting | bytes 4194304 | tf_op jit(solution)/shard_map/reshape | solution.py:100
  635.2 73.6 %reshape_reshape.3 = bf16[4,2,4,32,8,4,32]{6,5,4,3,2,1,0:T(4,128)(2,1)} reshape(bf16[4,64,4,256,4]{4,3,2,1,0:T(8,128)(2,1)} %bitcast.37) | data formatting | bytes 4194304 | tf_op jit(solution)/shard_map/reshape;reshape | solution.py:105
  708.8 12.0 %copy.44 = bf16[4,2,8,4,4,32,32]{6,5,4,3,0,2,1:T(8,128)(2,1)} copy(bf16[4,2,8,4,4,32,32]{6,4,2,5,3,1,0:T(4,128)(2,1)} %bitcast.191) | data formatting | bytes 4194304 | tf_op jit(solution)/shard_map/reshape | solution.py:106
  720.8 11.4 %reshape.93 = bf16[4,16,16,1024]{3,2,0,1:T(8,128)(2,1)S(1)} reshape(bf16[4,2,8,4,4,32,32]{6,5,4,3,0,2,1:T(8,128)(2,1)} %copy.44) | data formatting | bytes 4194304 | tf_op jit(solution)/shard_map/reshape | solution.py:106
  740.1 17.9 %all-reduce.5 = f32[4,4,4,192]{3,0,2,1:T(4,128)S(1)} all-reduce(f32[4,4,4,192]{3,0,2,1:T(4,128)S(1)} %fusion.57), channel_id=2, replica_groups=mesh['field'=2,'tm'=4,'tile'=4] {'tile'}, use_global_device_ids=true, to_apply=%region_9.10.clone | all-reduce | flops 12288 | bytes 98304
  (99 shorter events, 212.4 us)
Async XLA Ops:
  6.5 725.6 %all-gather.2.cloned.1.call-start = ((), (), s32[]{:S(2)}) async-start(), calls=%async_computation.1 | async-start | bytes 2621440 | tf_op jit(solution)/shard_map/all_gather | solution.py:116
  208.3 7.1 copy-start.12
  208.3 7.1 copy-start.13
  215.4 16.4 %copy-start.2 = (bf16[2,9,64,64]{3,2,1,0:T(8,128)(2,1)S(1)}, bf16[2,9,64,64]{3,2,1,0:T(8,128)(2,1)}, u32[]{:S(2)}) copy-start(bf16[2,9,64,64]{3,2,1,0:T(8,128)(2,1)} %param.21) | copy-start | bytes 442372
  215.5 17.2 %copy-start.11 = (f32[2,64]{1,0:T(2,128)S(1)}, f32[2,64]{1,0:T(2,128)}, u32[]{:S(2)}) copy-start(f32[2,64]{1,0:T(2,128)} %param.22) | copy-start | bytes 1540
  224.1 20.8 %copy-start = (bf16[4,64,256,16]{2,3,1,0:T(8,128)(2,1)}, bf16[4,64,256,16]{2,3,1,0:T(8,128)(2,1)S(1)}, u32[]{:S(2)}) copy-start(bf16[4,64,256,16]{2,3,1,0:T(8,128)(2,1)S(1)} %get-tuple-element.462) | copy-start | bytes 6291460
  225.4 7.8 %collective-permute-start = (bf16[4,1,256,64]{2,3,1,0:T(8,128)(2,1)S(1)}, bf16[4,1,256,64]{2,3,1,0:T(8,128)(2,1)S(1)}, u32[]{:S(2)}, u32[]{:S(2)}) collective-permute-start(bf16[4,1,256,64]{2,3,1,0:T(8,128)(2,1)S(1)} %get-tuple-element.233), channel_id=1, source_target_pairs={{0,1},{1,2},{2,3},{4,5},{5,6},{6,7},{8,9},{9,10},{10,11},{12,13},{... | collective-permute-start | bytes 393224 | tf_op jit(solution)/shard_map/ppermute | solution.py:14
  230.3 6.9 collective-permute-start.1
  249.2 159.8 %copy-start.7 = (s32[16,64]{1,0:T(8,128)S(1)}, s32[16,64]{1,0:T(8,128)}, u32[]{:S(2)}) copy-start(s32[16,64]{1,0:T(8,128)} %param.26) | copy-start | bytes 12292
  249.2 160.5 %copy-start.1 = (bf16[1,9,64,64]{3,2,1,0:T(8,128)(2,1)S(1)}, bf16[1,9,64,64]{3,2,1,0:T(8,128)(2,1)}, u32[]{:S(2)}) copy-start(bf16[1,9,64,64]{3,2,1,0:T(8,128)(2,1)} %get-tuple-element.235) | copy-start | bytes 221188
  249.2 160.7 %copy-start.8 = (s32[16,64]{1,0:T(8,128)S(1)}, s32[16,64]{1,0:T(8,128)}, u32[]{:S(2)}) copy-start(s32[16,64]{1,0:T(8,128)} %param.25) | copy-start | bytes 12292
  249.2 161.3 %copy-start.14 = (u32[32]{0:T(128)S(1)}, u32[32]{0:T(128)}, u32[]{:S(2)}) copy-start(u32[32]{0:T(128)} %constant.74) | copy-start | bytes 388
  404.2 7.6 collective-permute-start.2
  407.5 6.9 collective-permute-start.3
  421.8 4.3 copy-start.5
  426.1 153.9 %copy-start.4 = (bf16[64,16]{0,1:T(8,128)(2,1)S(1)}, bf16[64,16]{0,1:T(8,128)(2,1)}, u32[]{:S(2)}) copy-start(bf16[64,16]{0,1:T(8,128)(2,1)} %param.23) | copy-start | bytes 6148
  720.8 11.4 %copy-start.3 = (f32[16,64,16]{1,2,0:T(8,128)S(1)}, f32[16,64,16]{1,2,0:T(8,128)}, u32[]{:S(2)}) copy-start(f32[16,64,16]{1,2,0:T(8,128)} %fusion.72) | copy-start | bytes 196612
  720.8 13.8 %copy-start.6 = (s32[4,4,192]{2,1,0:T(4,128)S(1)}, s32[4,4,192]{2,1,0:T(4,128)}, u32[]{:S(2)}) copy-start(s32[4,4,192]{2,1,0:T(4,128)} %multiply_add_fusion) | copy-start | bytes 36868
  720.8 13.8 %copy-start.9 = (s32[1024]{0:T(1024)S(1)}, s32[1024]{0:T(1024)}, u32[]{:S(2)}) copy-start(s32[1024]{0:T(1024)} %eq.59) | copy-start | bytes 12292
  720.8 44.4 %copy-start.10 = (f32[192]{0:T(256)S(1)}, f32[192]{0:T(256)}, u32[]{:S(2)}) copy-start(f32[192]{0:T(256)} %param.27) | copy-start | bytes 2308
Sparse Core Ops, SparseCore 0:
  232.0 24.8 all-gather.1
where the time goes:
time: 777 us; the launch traced here: 773 us
  local copies, waits for them, and re-layouts  402 us (52%)
  matrix products  240 us (31%)
  other arithmetic  74.1 us (10%)
  blocking collectives  24.4 us (3%)
  between operations  13.6 us (2%)
  starting transfers between devices  11.3 us (1%)
    reshape x1, local copies, waits for them, and re-layouts, body(): movie.reshape(frame_count, coarse_rows, 4, coarse_cols, 4)  146 us
    dot_general x8, matrix products, single(): jnp.einsum('rwc,cn->rwn', frame[2:2 + rows_out], stacked_weights[2], pref...  85.6 us
    another operation x1, local copies, waits for them, and re-layouts, body(): denoised.reshape(frame_count, block_rows, 4, win, block_cols, 4, win)  73.6 us
    dot_general x8, matrix products, single(): jnp.einsum('rwc,cn->rwn', frame[0:rows_out], stacked_weights[0], preferre...  63.6 us
    dot_general x8, matrix products, single(): jnp.einsum('rwc,cn->rwn', frame[1:1 + rows_out], stacked_weights[1], pref...  63.2 us
    dynamic_update_slice x8, other arithmetic, body(): features = lax.map(embed, raw)  57 us
    transpose x1, local copies, waits for them, and re-layouts, body(): movie.reshape(frame_count, coarse_rows, 4, coarse_cols, 4)  55.9 us
    reshape x2, local copies, waits for them, and re-layouts, body(): decoded.reshape(frame_count, coarse_rows, coarse_cols, 4, 4)  43.7 us
  transfers between devices with their start and end apart: 5, of which 2 were waited for; matrix products, arithmetic and copies ran while one was open for 63% of the time, Pallas kernels for 0%

commit v1 on v0

v1 whole, which is shorter than its diff:
```python
import functools

import jax
import jax.numpy as jnp
from jax import lax
from jax.experimental import pallas as pl
from jax.experimental.pallas import tpu as pltpu
from jax.sharding import PartitionSpec as P

BLK = 128
LANES = 128
STRIP = 8
NT = (((1,), (1,)), ((), ()))
F32 = jnp.float32
BF16 = jnp.bfloat16


def conv_taps(layer):
    blocks = []
    for d in range(2):
        for side in range(2):
            for x in range(2):
                for h_in in range(2):
                    in_row = 2 * (d - 1) + h_in if layer % 2 == 0 else 2 * d - h_in
                    in_col = x if side == 0 else (-1, 2)[x]
                    row = []
                    for c in range(2):
                        for h_out in range(2):
                            out_row = -h_out if layer % 2 == 0 else h_out
                            tap_r, tap_c = in_row - out_row + 1, in_col - c + 1
                            ok = 0 <= tap_r <= 2 and 0 <= tap_c <= 2
                            row.append(3 * tap_r + tap_c if ok else None)
                    blocks.append(row)
    return blocks


def prep_kernel(patch_in_ref, conv_ref, patch_out_ref, win_ref, w1_ref, w2_ref, wd_ref):
    chan = patch_in_ref.shape[1]
    pixel = lax.broadcasted_iota(jnp.int32, (256, 16), 0)
    tap = lax.broadcasted_iota(jnp.int32, (256, 16), 1)
    sel = (((pixel // 32) % 4) * 4 + pixel % 4 == tap).astype(BF16)
    spread_in = jnp.dot(sel, patch_in_ref[...], preferred_element_type=F32)
    spread_out = lax.dot_general(patch_out_ref[...], sel, NT, preferred_element_type=F32)
    k = lax.broadcasted_iota(jnp.int32, (256, 2 * chan), 0)
    lane = lax.broadcasted_iota(jnp.int32, (256, 2 * chan), 1)
    wide_in = jnp.concatenate([spread_in, spread_in], axis=1)
    for pair in range(8):
        keep = ((k % 32) // 4 == pair) & (k // 128 == lane // chan)
        win_ref[:, pair * 2 * chan : (pair + 1) * 2 * chan] = jnp.where(keep, wide_in, 0.0).astype(BF16)
    k = lax.broadcasted_iota(jnp.int32, (2 * chan, 256), 1)
    half = lax.broadcasted_iota(jnp.int32, (2 * chan, 256), 0) // chan
    wide_out = jnp.concatenate([spread_out, spread_out], axis=0)
    for pair in range(8):
        keep = ((k % 32) // 4 == pair) & (k // 128 == half)
        wd_ref[pair * 2 * chan : (pair + 1) * 2 * chan, :] = jnp.where(keep, wide_out, 0.0).astype(BF16)
    eye = (
        lax.broadcasted_iota(jnp.int32, (chan, chan), 0)
        == lax.broadcasted_iota(jnp.int32, (chan, chan), 1)
    ).astype(BF16)
    blank = jnp.zeros((chan, chan), F32)
    for layer, out in enumerate((w1_ref, w2_ref)):
        turned = [
            lax.dot_general(eye, conv_ref[layer, tap], NT, preferred_element_type=F32)
            for tap in range(9)
        ]
        for row, taps in enumerate(conv_taps(layer)):
            for c in range(2):
                pair = [blank if taps[2 * c + h] is None else turned[taps[2 * c + h]] for h in range(2)]
                out[row * chan : (row + 1) * chan, c * LANES : (c + 1) * LANES] = jnp.concatenate(
                    pair, axis=1
                ).astype(BF16)


def prepare(patch_in, conv_weight, patch_out):
    chan = patch_in.shape[1]
    return pl.pallas_call(
        prep_kernel,
        out_shape=(
            jax.ShapeDtypeStruct((256, 16 * chan), BF16),
            jax.ShapeDtypeStruct((16 * chan, 4 * chan), BF16),
            jax.ShapeDtypeStruct((16 * chan, 4 * chan), BF16),
            jax.ShapeDtypeStruct((16 * chan, 256), BF16),
        ),
        name="prep",
    )(patch_in, conv_weight, patch_out)


def store_features(lo_ref, hi_ref, base, first, lo, hi, frames, rows):
    count = lo.shape[0] // rows
    lo_ref[base, first * rows : (first + count) * rows, :] = lo.astype(BF16)
    hi_ref[base, (first + 1) * rows : (first + count + 1) * rows, :] = hi.astype(BF16)
    group = lax.broadcasted_iota(jnp.int32, (rows, LANES), 0) % (rows // frames)
    if first == 0:
        up = pltpu.roll(lo[0:rows], rows - 1, 0)
        up = jnp.where(group == rows // frames - 1, 0.0, up)
        lo_ref[base, 16 * rows : 17 * rows, :] = up.astype(BF16)
    if first + count == 16:
        down = pltpu.roll(hi[(count - 1) * rows : count * rows], 1, 0)
        down = jnp.where(group == 0, 0.0, down)
        hi_ref[base, 0:rows, :] = down.astype(BF16)


def gather_rows(lo_ref, hi_ref, base, start, size, rows):
    a, b = start, start + size
    return [
        lo_ref[base, a:b, :],
        hi_ref[base, a + rows : b + rows, :],
        hi_ref[base, a:b, :],
        lo_ref[base, a + rows : b + rows, :],
    ]


def denoise_kernel(
    strips,
    frames,
    masked,
    flags_ref,
    movie_ref,
    win_ref,
    w1_ref,
    w2_ref,
    wd_ref,
    patch_bias_ref,
    conv_bias_ref,
    out_ref,
    z_ref,
    x_ref,
    f0lo_ref,
    f0hi_ref,
    f1lo_ref,
    f1hi_ref,
):
    blocks = movie_ref.shape[2] // LANES
    rows = frames * blocks
    m = 16 * rows
    lane = lax.broadcasted_iota(jnp.int32, (rows, LANES), 1)
    odd_chunk = (lane // 32) % 2 == 1
    high_chunk = lane // 64 == 1
    step = pl.program_id(0)

    for ref in (f0lo_ref, f0hi_ref, f1lo_ref, f1hi_ref, x_ref):
        ref[0] = ref[strips]

    scale = [None] * strips
    odd_scale = [None] * strips
    even_scale = [None] * strips
    if masked:
        first = step == 0
        last = step == pl.num_programs(0) - 1
        top = jnp.where(first, flags_ref[0], 1.0)
        bottom = jnp.where(last, flags_ref[1], 1.0)
        scale[0] = top
        scale[strips - 1] = bottom
        odd_scale[strips - 1] = top
        even_scale[strips - 1] = bottom

    for s in range(strips):
        for f in range(frames):
            pixels = movie_ref[f, s * STRIP : (s + 1) * STRIP, :].astype(F32)
            for t in range(blocks):
                z_ref[s, (f * blocks + t) * STRIP : (f * blocks + t + 1) * STRIP, :] = pixels[
                    :, t * LANES : (t + 1) * LANES
                ]
    for s in range(strips):
        halves = []
        for g in range(2):
            a = [z_ref[s, pl.ds(4 * g + p, rows, stride=STRIP), :] for p in range(4)]
            b = [None] * 4
            for p in (0, 2):
                b[p] = jnp.where(odd_chunk, pltpu.roll(a[p + 1], 32, 1), a[p])
                b[p + 1] = jnp.where(odd_chunk, a[p + 1], pltpu.roll(a[p], LANES - 32, 1))
            c = [None] * 4
            for p in (0, 1):
                c[p] = jnp.where(high_chunk, pltpu.roll(b[p + 2], 64, 1), b[p])
                c[p + 2] = jnp.where(high_chunk, b[p + 2], pltpu.roll(b[p], LANES - 64, 1))
            halves.append(c)
        for q in range(4):
            x_ref[s + 1, q * rows : (q + 1) * rows, 0:LANES] = halves[0][q].astype(BF16)
            x_ref[s + 1, q * rows : (q + 1) * rows, LANES : 2 * LANES] = halves[1][q].astype(BF16)

    for s in range(strips):
        summed = jnp.dot(x_ref[s + 1], win_ref[...], preferred_element_type=F32)
        bias = patch_bias_ref[...]
        for q in range(4):
            for j in range(4):
                part = summed[q * rows : (q + 1) * rows, j * 256 : (j + 1) * 256]
                part = jnp.maximum(part + bias, 0.0)
                if scale[s] is not None:
                    part = part * scale[s]
                store_features(
                    f0lo_ref, f0hi_ref, s + 1, 4 * q + j, part[:, 0:LANES], part[:, LANES:], frames, rows
                )

    lane_m = lax.broadcasted_iota(jnp.int32, (m, LANES), 1) < 64

    for s in range(strips):
        pieces = gather_rows(f0lo_ref, f0hi_ref, s, 0, m, rows) + gather_rows(
            f0lo_ref, f0hi_ref, s + 1, 0, m, rows
        )
        summed = jnp.dot(
            jnp.concatenate(pieces, axis=1), w1_ref[...], preferred_element_type=F32
        )
        summed = jnp.maximum(summed + conv_bias_ref[0:1, :], 0.0)
        new = []
        for c in range(2):
            kept = jnp.where(lane_m, pieces[4 + c].astype(F32), pieces[c].astype(F32))
            value = kept + summed[:, c * LANES : (c + 1) * LANES]
            if even_scale[s] is not None:
                value = value * jnp.where(lane_m, even_scale[s], odd_scale[s])
            new.append(value)
        store_features(f1lo_ref, f1hi_ref, s + 1, 0, new[0], new[1], frames, rows)

    for s in range(strips):
        pieces = gather_rows(f1lo_ref, f1hi_ref, s, 0, m, rows) + gather_rows(
            f1lo_ref, f1hi_ref, s + 1, 0, m, rows
        )
        summed = jnp.dot(
            jnp.concatenate(pieces, axis=1), w2_ref[...], preferred_element_type=F32
        )
        summed = jnp.maximum(summed + conv_bias_ref[1:2, :], 0.0)
        new = []
        for c in range(2):
            kept = jnp.where(lane_m, pieces[c].astype(F32), pieces[4 + c].astype(F32))
            new.append((kept + summed[:, c * LANES : (c + 1) * LANES]).astype(BF16))
        wide = []
        for q in range(4):
            parts = []
            for j in range(4):
                at = (4 * q + j) * rows
                parts += [new[0][at : at + rows], new[1][at : at + rows]]
            wide.append(jnp.concatenate(parts, axis=1))
        decoded = jnp.dot(
            jnp.concatenate(wide, axis=0), wd_ref[...], preferred_element_type=F32
        )
        out_ref[s] = (decoded + x_ref[s].astype(F32)).astype(BF16)


def denoise(movie, flags, weights, patch_bias, conv_bias, strips, masked, name):
    frames, height, width = movie.shape
    total = height // STRIP
    rows = frames * (width // LANES)
    grid = total // strips
    win, w1, w2, wd = weights
    whole = lambda a: pl.BlockSpec(a.shape, lambda n: (0,) * a.ndim)
    flops = 2 * total * rows * 16 * (2 * 1024 * 256 + 256 * 256 + 256 * 256)
    return pl.pallas_call(
        functools.partial(denoise_kernel, strips, frames, masked),
        grid=(grid,),
        in_specs=[
            pl.BlockSpec(memory_space=pltpu.SMEM),
            pl.BlockSpec((frames, strips * STRIP, width), lambda n: (0, n, 0)),
            whole(win),
            whole(w1),
            whole(w2),
            whole(wd),
            whole(patch_bias),
            whole(conv_bias),
        ],
        out_specs=pl.BlockSpec((strips, 4 * rows, 256), lambda n: (n, 0, 0)),
        out_shape=jax.ShapeDtypeStruct((total, 4 * rows, 256), BF16),
        scratch_shapes=[
            pltpu.VMEM((strips, rows * STRIP, LANES), F32),
            pltpu.VMEM((strips + 1, 4 * rows, 256), BF16),
        ]
        + [pltpu.VMEM((strips + 1, 17 * rows, LANES), BF16)] * 4,
        compiler_params=pltpu.CompilerParams(vmem_limit_bytes=48 << 20),
        cost_estimate=pl.CostEstimate(flops=flops, bytes_accessed=8 << 20, transcendentals=0),
        name=name,
    )(flags, movie, win, w1, w2, wd, patch_bias, conv_bias)


def cells_kernel(frames, own, inner_ref, edge_ref, footprint_ref, cell_ref, window_ref, out_ref):
    total = inner_ref.shape[0]
    rows4 = inner_ref.shape[1]
    rows = rows4 // 4
    blocks = rows // frames
    slots = footprint_ref.shape[1]
    n = blocks * slots
    owned = out_ref.shape[0]
    group = lax.broadcasted_iota(jnp.int32, (blocks, n), 0)
    acc = None
    for kb in range(total // 16):
        lhs = []
        for iw in range(4):
            parts = []
            for i4 in range(4):
                i = 16 * kb + 4 * iw + i4
                if i == 0:
                    parts.append(edge_ref[2])
                elif i == total - 1:
                    parts.append(edge_ref[5])
                else:
                    parts.append(inner_ref[i + 1])
            lhs.append(jnp.concatenate(parts, axis=1))
        weights = footprint_ref[kb * blocks : (kb + 1) * blocks].reshape(n, footprint_ref.shape[2])
        every = lax.dot_general(
            jnp.concatenate(lhs, axis=0), weights, NT, preferred_element_type=F32
        )
        block_of = lax.broadcasted_iota(jnp.int32, (1, n), 1) // slots
        target = window_ref[kb : kb + 1, :] * blocks + block_of
        sums = []
        for f in range(frames):
            total_f = jnp.zeros((blocks, n), F32)
            for w in range(16):
                at = w * rows + f * blocks
                total_f = total_f + jnp.where(
                    target == group + w * blocks, every[at : at + blocks, :], 0.0
                )
            sums.append(jnp.sum(total_f, axis=0, keepdims=True))
        slot_sums = jnp.concatenate(sums, axis=0)
        cell = cell_ref[kb : kb + 1, :]
        owner = jnp.floor((cell.astype(F32) + 0.5) * (1.0 / own)).astype(jnp.int32)
        low = cell - owner * own
        row_owner = lax.broadcasted_iota(jnp.int32, (owned, n), 0) // frames
        onehot = jnp.where(
            lax.broadcasted_iota(jnp.int32, (own, n), 0) == low, 1.0, 0.0
        ).astype(BF16)
        spread = jnp.where(
            row_owner == owner, jnp.concatenate([slot_sums] * (owned // frames), axis=0), 0.0
        )
        for _ in range(3):
            piece = spread.astype(BF16)
            spread = spread - piece.astype(F32)
            part = lax.dot_general(piece, onehot, NT, preferred_element_type=F32)
            acc = part if acc is None else acc + part
    out_ref[...] = acc


def cells(inner, edge, footprint, slot_cell, window, frames, own, owners):
    blocks = inner.shape[1] // (4 * frames)
    return pl.pallas_call(
        functools.partial(cells_kernel, frames, own),
        out_shape=jax.ShapeDtypeStruct((owners * frames, own), F32),
        compiler_params=pltpu.CompilerParams(vmem_limit_bytes=48 << 20),
        cost_estimate=pl.CostEstimate(flops=2 << 30, bytes_accessed=5 << 20, transcendentals=0),
        name="cells",
    )(inner, edge, footprint, slot_cell.reshape(-1, blocks * slot_cell.shape[1]),
      window.reshape(-1, blocks * window.shape[1]))


def spikes_kernel(tm, tile, frames, moved_ref, decay_ref, out_ref):
    own = out_ref.shape[1]
    pieces = []
    for a in range(tm):
        total = jnp.zeros((frames, own), F32)
        for b in range(tile):
            at = (a * tile + b) * frames
            total = total + moved_ref[at : at + frames, :]
        pieces.append(total)
    traces = jnp.concatenate(pieces, axis=0)
    count = tm * frames
    centered = traces - jnp.sum(traces, axis=0, keepdims=True) * (1.0 / count)
    previous = jnp.concatenate([jnp.zeros((1, own), F32), centered[:-1]], axis=0)
    spikes = centered - decay_ref[...] * previous
    power = jnp.sum(spikes * spikes, axis=0, keepdims=True) * (1.0 / count)
    out_ref[...] = spikes / jnp.sqrt(power + 1e-05)


def body(
    movie,
    patch_in,
    patch_bias,
    conv_weight,
    conv_bias,
    patch_out,
    footprint,
    slot_cell,
    slot_window_index,
    decay,
):
    frames = movie.shape[0]
    own = decay.shape[0]
    tm, tile = lax.axis_size("tm"), lax.axis_size("tile")
    place = lax.axis_index("tile")
    forward = [(i, i + 1) for i in range(tile - 1)]
    backward = [(target, source) for source, target in forward]
    above = lax.ppermute(movie[:, -STRIP:], "tile", forward)
    below = lax.ppermute(movie[:, :STRIP], "tile", backward)
    slots = lax.all_gather(footprint, "tm", axis=1, tiled=True)
    weights = prepare(patch_in, conv_weight, patch_out)
    bias0 = jnp.tile(patch_bias[None, :], (1, 4))
    bias12 = jnp.tile(conv_bias, (1, 4))
    flags = jnp.stack([place > 0, place < tile - 1]).astype(F32)
    inner = denoise(movie, flags, weights, bias0, bias12, 2, False, "inner")
    rim = jnp.concatenate(
        [above, movie[:, : 2 * STRIP], movie[:, -2 * STRIP :], below], axis=1
    )
    edge = denoise(rim, flags, weights, bias0, bias12, 2, True, "edge")
    per_cell = cells(inner, edge, slots, slot_cell, slot_window_index, frames, own, tm * tile)
    moved = lax.all_to_all(per_cell, ("tm", "tile"), split_axis=0, concat_axis=0, tiled=True)
    return pl.pallas_call(
        functools.partial(spikes_kernel, tm, tile, frames),
        out_shape=jax.ShapeDtypeStruct((tm * frames, own), F32),
        name="spikes",
    )(moved, decay[None, :])


def solution(mesh):
    placed = (
        P(("field", "tm"), "tile", None),
        P(),
        P(),
        P(),
        P(),
        P(),
        P(("field", "tile"), "tm", None),
        P(("field", "tile"), None),
        P(("field", "tile"), None),
        P(("field", "tm", "tile")),
    )
    return jax.shard_map(
        body,
        mesh=mesh,
        in_specs=placed,
        out_specs=P(None, ("field", "tm", "tile")),
        check_vma=False,
    )
```

time: 777 us -> 105 us (0.14)
  local copies, waits for them, and re-layouts: 402 us -> 14.2 us
  matrix products: 240 us -> 0 us
  other arithmetic: 74.1 us -> 0.1 us
  Pallas kernels: 0 us -> 56.5 us
  blocking collectives: 24.4 us -> 13.4 us
    dot_general x34 -> x0, matrix products: 240 us -> none  [the longest x8 85.6 us: single(): jnp.einsum('rwc,cn->rwn', frame[2:2 + rows_out], stacked_weights[2], pref...]
    reshape x7 -> x2, local copies, waits for them, and re-layouts: 213 us -> 0.15 us  [the longest x1 0.08 us: cells(): slot_cell.reshape(-1, blocks * slot_cell.shape[1])]
    another operation x4, local copies, waits for them, and re-layouts: 86.5 us -> 1.51 us  [the longest x2 0.76 us: body(): bias12 = jnp.tile(conv_bias, (1, 4))]
    dynamic_update_slice x8 -> x0, other arithmetic: 57 us -> none  [body(): features = lax.map(embed, raw)]
    pallas_call x0 -> x5, Pallas kernels: none -> 56.5 us  [the longest x2 50 us: denoise(): pl.pallas_call(functools.partial(denoise_kernel, strips, frames, masked),...]
    transpose x1 -> x0, local copies, waits for them, and re-layouts: 55.9 us -> none  [body(): movie.reshape(frame_count, coarse_rows, 4, coarse_cols, 4)]
    slice x12 -> x2, local copies, waits for them, and re-layouts: 41.7 us -> 1.87 us  [the longest x1 0.99 us: body(): movie[:, :2 * STRIP]]
    unnamed x1 -> x0, blocking collectives: 17.9 us -> none
  transfers between devices with their start and end apart: 5 -> 3, of which waited for: 2 -> 0; matrix products, arithmetic and copies ran while one was open for 63% -> 5% of each run, Pallas kernels for 0% -> 50%
where the time goes in v1:
time: 105 us
  Pallas kernels  56.5 us (54%)
  local copies, waits for them, and re-layouts  14.2 us (14%)
  between operations  13.5 us (13%)
  blocking collectives  13.4 us (13%)
  starting transfers between devices  6.23 us (6%)
    pallas_call x2, Pallas kernels, denoise(): pl.pallas_call(functools.partial(denoise_kernel, strips, frames, masked),...  50 us
    all_to_all x1, blocking collectives, body(): lax.all_to_all(per_cell, ('tm', 'tile'), split_axis=0, concat_axis=0, til...  13.4 us
    unnamed x27, local copies, waits for them, and re-layouts  10 us
    ppermute x1, starting transfers between devices, body(): above = lax.ppermute(movie[:, -STRIP:], 'tile', forward)  4.93 us
    pallas_call x1, Pallas kernels, prepare(): pl.pallas_call(prep_kernel, out_shape=(jax.ShapeDtypeStruct((256, 16 * ch...  2.62 us
    pallas_call x1, Pallas kernels, cells(): pl.pallas_call(functools.partial(cells_kernel, frames, own), out_shape=ja...  2.33 us
  transfers between devices with their start and end apart: 3, of which 0 were waited for; matrix products, arithmetic and copies ran while one was open for 5% of the time, Pallas kernels for 50%

profile of v1, /device:TPU:0, one launch (start us, length us, event | category | flops | bytes accessed | tf_op | source)
XLA Modules:
  0.0 104.7 jit_solution(13248254276282701247)
XLA Ops:
  6.5 0.0 all-gather.2.cloned.1.call-start
  6.5 0.7 all-gather.2.cloned.1.call-update
  7.3 0.9 fusion
  8.1 4.9 %collective-permute-start = (bf16[4,8,1024]{2,1,0:T(8,128)(2,1)S(1)}, bf16[4,8,1024]{2,1,0:T(8,128)(2,1)S(1)}, u32[]{:S(2)}, u32[]{:S(2)}) collective-permute-start(bf16[4,8,1024]{2,1,0:T(8,128)(2,1)S(1)} %get-tuple-element.13), channel_id=1, source_target_pairs={{0,1},{1,2},{2,3},{4,5},{5,6},{6,7},{8,9},{9,10},{10,11},{12,13},{... | collective-permute-start | bytes 196616 | tf_op jit(solution)/shard_map/ppermute | solution.py:377
  13.1 1.3 %collective-permute-start.1 = (bf16[4,8,1024]{2,1,0:T(8,128)(2,1)S(1)}, bf16[4,8,1024]{2,1,0:T(8,128)(2,1)S(1)}, u32[]{:S(2)}, u32[]{:S(2)}) collective-permute-start(bf16[4,8,1024]{2,1,0:T(8,128)(2,1)S(1)} %get-tuple-element.14), channel_id=1, source_target_pairs={{1,0},{2,1},{3,2},{5,4},{6,5},{7,6},{9,8},{10,9},{11,10},{13,12},{... | collective-permute-start | bytes 196616 | tf_op jit(solution)/shard_map/ppermute | solution.py:378
  14.4 1.4 %copy.11.patch_out_ref = bf16[64,16]{1,0:T(8,128)(2,1)} copy(bf16[64,16]{0,1:T(8,128)(2,1)} %param.15) | data formatting | bytes 4096 | tf_op args[5]
  15.8 0.7 tile.19
  16.4 0.1 tile.20.conv_bias_ref
  16.5 0.7 tile.8
  17.2 0.1 tile.18.patch_bias_ref
  17.3 2.6 %prep.1 = (bf16[256,1024]{1,0:T(8,128)(2,1)}, bf16[1024,256]{1,0:T(8,128)(2,1)}, bf16[1024,256]{1,0:T(8,128)(2,1)}, bf16[1024,256]{1,0:T(8,128)(2,1)}) custom-call(bf16[16,64]{1,0:T(8,128)(2,1)} %patch_in_ref.1, bf16[2,9,64,64]{3,2,1,0:T(8,128)(2,1)} %conv_ref.1, bf16[64,16]{1,0:T(8,128)(2,1)} %copy.11.patch_out_ref), custom_call_target="tpu_custom_call" | custom-call | tf_op jit(solution)/shard_map/prep/pallas_call | solution.py:76
  19.9 0.1 add_convert_fusion.flags_ref
  20.0 1.0 copy-done.1
  21.0 1.0 copy-done.3
  22.1 1.0 copy-done.5
  23.1 1.0 copy-done.7
  24.2 41.7 %inner.1.inner_ref = bf16[32,128,256]{2,1,0:T(8,128)(2,1)S(1)} custom-call(f32[2]{0:T(128)S(1)} %add_convert_fusion.flags_ref, bf16[4,256,1024]{2,1,0:T(8,128)(2,1)} %movie_ref.1, bf16[256,1024]{1,0:T(8,128)(2,1)S(1)} %copy-done.1, bf16[1024,256]{1,0:T(8,128)(2,1)S(1)} %copy-done.3, bf16[1024,256]{1,0:T(8,128)(2,1)S(1)} %copy-done.5, ...), custom_call_target="tpu_custom_call" | custom-call | flops 21474836480 | bytes 8388608 | tf_op jit(solution)/shard_map/inner/pallas_call | solution.py:246
  65.8 1.3 %copy-done.9 = bf16[32,128,256]{2,1,0:T(8,128)(2,1)} copy-done((bf16[32,128,256]{2,1,0:T(8,128)(2,1)}, bf16[32,128,256]{2,1,0:T(8,128)(2,1)S(1)}, u32[]{:S(2)}) %copy-start.9) | copy-done | bytes 2097176
  67.1 1.0 fusion.1
  68.1 0.1 reshape.18.cell_ref
  68.2 0.0 copy-done.12
  68.2 0.1 reshape.19.window_ref
  68.3 0.0 collective-permute-done
  68.3 0.0 collective-permute-done.1
  68.4 8.3 %edge.1.edge_ref = bf16[6,128,256]{2,1,0:T(8,128)(2,1)S(1)} custom-call(f32[2]{0:T(128)S(1)} %add_convert_fusion.flags_ref, bf16[4,48,1024]{2,1,0:T(8,128)(2,1)S(1)} %pad_maximum_fusion.movie_ref, bf16[256,1024]{1,0:T(8,128)(2,1)S(1)} %copy-done.2, bf16[1024,256]{1,0:T(8,128)(2,1)S(1)} %copy-done.4, bf16[1024,256]{1,0:T(8,128)(2,1)S(1)} %copy-done.6, ...), custom_call_target="tpu_custom_call" | custom-call | flops 4026531840 | bytes 8388608 | tf_op jit(solution)/shard_map/edge/pallas_call | solution.py:246
  76.7 0.0 all-gather.2.cloned.1.call-done.footprint_ref
  76.8 1.6 %copy-done = bf16[16,64,1024]{2,1,0:T(8,128)(2,1)S(1)} copy-done((bf16[16,64,1024]{2,1,0:T(8,128)(2,1)S(1)}, bf16[16,64,1024]{2,1,0:T(8,128)(2,1)}, u32[]{:S(2)}) %copy-start) | copy-done | bytes 2097176
  78.4 1.6 %copy-done.10 = bf16[32,128,256]{2,1,0:T(8,128)(2,1)S(1)} copy-done((bf16[32,128,256]{2,1,0:T(8,128)(2,1)S(1)}, bf16[32,128,256]{2,1,0:T(8,128)(2,1)}, u32[]{:S(2)}) %copy-start.10) | copy-done | bytes 2097176
  80.0 2.3 %cells.1 = f32[64,192]{1,0:T(8,128)S(1)} custom-call(bf16[32,128,256]{2,1,0:T(8,128)(2,1)S(1)} %copy-done.10, bf16[6,128,256]{2,1,0:T(8,128)(2,1)S(1)} %edge.1.edge_ref, bf16[16,64,1024]{2,1,0:T(8,128)(2,1)S(1)} %copy-done, s32[2,512]{1,0:T(2,128)S(1)} %reshape.18.cell_ref, s32[2,512]{1,0:T(2,128)S(1)} %reshape.19.window_ref), custom_call_target="tpu_custom_call" | custom-call | flops 2147483648 | bytes 5242880 | tf_op jit(solution)/shard_map/cells/pallas_call | solution.py:331
  82.3 13.4 %all_to_all.11 = f32[16,4,192]{2,1,0:T(4,128)S(1)} all-to-all(f32[16,4,192]{2,1,0:T(4,128)S(1)} %all_to_all.7), channel_id=1, replica_groups=mesh['field'=2,'tm'=4,'tile'=4] {'tm','tile'}, dimensions={0} | all-to-all | bytes 98304 | tf_op jit(solution)/shard_map/all_to_all | solution.py:390
  95.8 0.6 all_to_all.9.moved_ref
  96.4 1.5 %spikes.1 = f32[16,192]{1,0:T(8,128)} custom-call(f32[64,192]{1,0:T(8,128)} %all_to_all.9.moved_ref, f32[1,192]{1,0:T(1,128)} %bitcast.3), custom_call_target="tpu_custom_call" | custom-call | tf_op jit(solution)/shard_map/spikes/pallas_call | solution.py:391
  (20 shorter events, 0.1 us)
Async XLA Ops:
  6.5 70.2 %all-gather.2.cloned.1.call-start = ((), (), s32[]{:S(2)}) async-start(), calls=%async_computation.1 | async-start | bytes 2621440 | tf_op jit(solution)/shard_map/all_gather | solution.py:379
  8.1 60.2 %collective-permute-start = (bf16[4,8,1024]{2,1,0:T(8,128)(2,1)S(1)}, bf16[4,8,1024]{2,1,0:T(8,128)(2,1)S(1)}, u32[]{:S(2)}, u32[]{:S(2)}) collective-permute-start(bf16[4,8,1024]{2,1,0:T(8,128)(2,1)S(1)} %get-tuple-element.13), channel_id=1, source_target_pairs={{0,1},{1,2},{2,3},{4,5},{5,6},{6,7},{8,9},{9,10},{10,11},{12,13},{... | collective-permute-start | bytes 196616 | tf_op jit(solution)/shard_map/ppermute | solution.py:377
  13.1 55.2 %collective-permute-start.1 = (bf16[4,8,1024]{2,1,0:T(8,128)(2,1)S(1)}, bf16[4,8,1024]{2,1,0:T(8,128)(2,1)S(1)}, u32[]{:S(2)}, u32[]{:S(2)}) collective-permute-start(bf16[4,8,1024]{2,1,0:T(8,128)(2,1)S(1)} %get-tuple-element.14), channel_id=1, source_target_pairs={{1,0},{2,1},{3,2},{5,4},{6,5},{7,6},{9,8},{10,9},{11,10},{13,12},{... | collective-permute-start | bytes 196616 | tf_op jit(solution)/shard_map/ppermute | solution.py:378
  20.0 1.0 copy-start.1
  21.0 1.0 copy-start.3
  22.1 1.0 copy-start.5
  23.1 1.0 copy-start.7
  24.1 44.0 %copy-start.11 = (s32[16,64]{1,0:T(8,128)S(1)}, s32[16,64]{1,0:T(8,128)}, u32[]{:S(2)}) copy-start(s32[16,64]{1,0:T(8,128)} %param.17) | copy-start | bytes 12292
  24.1 44.1 %copy-start.12 = (s32[16,64]{1,0:T(8,128)S(1)}, s32[16,64]{1,0:T(8,128)}, u32[]{:S(2)}) copy-start(s32[16,64]{1,0:T(8,128)} %param.18) | copy-start | bytes 12292
  24.1 44.2 %copy-start.2 = (bf16[256,1024]{1,0:T(8,128)(2,1)S(1)}, bf16[256,1024]{1,0:T(8,128)(2,1)}, u32[]{:S(2)}) copy-start(bf16[256,1024]{1,0:T(8,128)(2,1)} %get-tuple-element.9.win_ref) | copy-start | bytes 1572868
  24.1 44.2 %copy-start.4 = (bf16[1024,256]{1,0:T(8,128)(2,1)S(1)}, bf16[1024,256]{1,0:T(8,128)(2,1)}, u32[]{:S(2)}) copy-start(bf16[1024,256]{1,0:T(8,128)(2,1)} %get-tuple-element.10.w1_ref) | copy-start | bytes 1572868
  24.1 44.2 %copy-start.6 = (bf16[1024,256]{1,0:T(8,128)(2,1)S(1)}, bf16[1024,256]{1,0:T(8,128)(2,1)}, u32[]{:S(2)}) copy-start(bf16[1024,256]{1,0:T(8,128)(2,1)} %get-tuple-element.11.w2_ref) | copy-start | bytes 1572868
  24.2 44.2 %copy-start.8 = (bf16[1024,256]{1,0:T(8,128)(2,1)S(1)}, bf16[1024,256]{1,0:T(8,128)(2,1)}, u32[]{:S(2)}) copy-start(bf16[1024,256]{1,0:T(8,128)(2,1)} %get-tuple-element.12.wd_ref) | copy-start | bytes 1572868
  65.8 1.3 %copy-start.9 = (bf16[32,128,256]{2,1,0:T(8,128)(2,1)}, bf16[32,128,256]{2,1,0:T(8,128)(2,1)S(1)}, u32[]{:S(2)}) copy-start(bf16[32,128,256]{2,1,0:T(8,128)(2,1)S(1)} %inner.1.inner_ref) | copy-start | bytes 6291460
  76.8 1.6 %copy-start = (bf16[16,64,1024]{2,1,0:T(8,128)(2,1)S(1)}, bf16[16,64,1024]{2,1,0:T(8,128)(2,1)}, u32[]{:S(2)}) copy-start(bf16[16,64,1024]{2,1,0:T(8,128)(2,1)} %all-gather.2.cloned.1.call-done.footprint_ref) | copy-start | bytes 6291460
  78.4 1.6 %copy-start.10 = (bf16[32,128,256]{2,1,0:T(8,128)(2,1)S(1)}, bf16[32,128,256]{2,1,0:T(8,128)(2,1)}, u32[]{:S(2)}) copy-start(bf16[32,128,256]{2,1,0:T(8,128)(2,1)} %copy-done.9) | copy-start | bytes 6291460
Sparse Core Ops, SparseCore 0:
  8.9 25.3 all-gather.1

commit v2 on v1

v2 whole, which is shorter than its diff:
```python
import functools

import jax
import jax.numpy as jnp
from jax import lax
from jax.experimental import pallas as pl
from jax.experimental.pallas import tpu as pltpu
from jax.sharding import PartitionSpec as P

BLK = 128
LANES = 128
STRIP = 8
STRIPS = 4
VMEM_BYTES = 60 << 20
NT = (((1,), (1,)), ((), ()))
F32 = jnp.float32
BF16 = jnp.bfloat16


def conv_taps(layer):
    blocks = []
    for d in range(2):
        for side in range(2):
            for x in range(2):
                for h_in in range(2):
                    in_row = 2 * (d - 1) + h_in if layer % 2 == 0 else 2 * d - h_in
                    in_col = x if side == 0 else (-1, 2)[x]
                    row = []
                    for c in range(2):
                        for h_out in range(2):
                            out_row = -h_out if layer % 2 == 0 else h_out
                            tap_r, tap_c = in_row - out_row + 1, in_col - c + 1
                            ok = 0 <= tap_r <= 2 and 0 <= tap_c <= 2
                            row.append(3 * tap_r + tap_c if ok else None)
                    blocks.append(row)
    return blocks


def prepare(patch_in_ref, conv_ref, patch_out_ref, win_ref, w1_ref, w2_ref, wd_ref):
    chan = patch_in_ref.shape[1]
    pixel = lax.broadcasted_iota(jnp.int32, (256, 16), 0)
    tap = lax.broadcasted_iota(jnp.int32, (256, 16), 1)
    sel = (((pixel // 32) % 4) * 4 + pixel % 4 == tap).astype(BF16)
    spread_in = jnp.dot(sel, patch_in_ref[...], preferred_element_type=F32)
    spread_out = lax.dot_general(patch_out_ref[...], sel, NT, preferred_element_type=F32)
    k = lax.broadcasted_iota(jnp.int32, (256, 2 * chan), 0)
    lane = lax.broadcasted_iota(jnp.int32, (256, 2 * chan), 1)
    wide_in = jnp.concatenate([spread_in, spread_in], axis=1)
    for pair in range(8):
        keep = ((k % 32) // 4 == pair) & (k // 128 == lane // chan)
        win_ref[:, pair * 2 * chan : (pair + 1) * 2 * chan] = jnp.where(keep, wide_in, 0.0).astype(BF16)
    k = lax.broadcasted_iota(jnp.int32, (2 * chan, 256), 1)
    half = lax.broadcasted_iota(jnp.int32, (2 * chan, 256), 0) // chan
    wide_out = jnp.concatenate([spread_out, spread_out], axis=0)
    for pair in range(8):
        keep = ((k % 32) // 4 == pair) & (k // 128 == half)
        wd_ref[pair * 2 * chan : (pair + 1) * 2 * chan, :] = jnp.where(keep, wide_out, 0.0).astype(BF16)
    eye = (
        lax.broadcasted_iota(jnp.int32, (chan, chan), 0)
        == lax.broadcasted_iota(jnp.int32, (chan, chan), 1)
    ).astype(BF16)
    blank = jnp.zeros((chan, chan), F32)
    for layer, out in enumerate((w1_ref, w2_ref)):
        turned = [
            lax.dot_general(eye, conv_ref[layer, tap], NT, preferred_element_type=F32)
            for tap in range(9)
        ]
        for row, taps in enumerate(conv_taps(layer)):
            for c in range(2):
                pair = [blank if taps[2 * c + h] is None else turned[taps[2 * c + h]] for h in range(2)]
                out[row * chan : (row + 1) * chan, c * LANES : (c + 1) * LANES] = jnp.concatenate(
                    pair, axis=1
                ).astype(BF16)


def denoise_kernel(
    strips,
    movie_ref,
    above_ref,
    below_ref,
    patch_in_ref,
    patch_bias_ref,
    conv_ref,
    conv_bias_ref,
    patch_out_ref,
    out_ref,
    win_ref,
    w1_ref,
    w2_ref,
    wd_ref,
    z_ref,
    x_ref,
    f0lo_ref,
    f0hi_ref,
    f1lo_ref,
    f1hi_ref,
    f2_ref,
):
    frames = movie_ref.shape[0]
    blocks = movie_ref.shape[2] // LANES
    rows = frames * blocks
    m = 16 * rows
    lane = lax.broadcasted_iota(jnp.int32, (rows, LANES), 1)
    group = lax.broadcasted_iota(jnp.int32, (rows, LANES), 0) % blocks
    odd_chunk = (lane // 32) % 2 == 1
    high_chunk = lane // 64 == 1
    step = pl.program_id(0)
    last = pl.num_programs(0) - 1
    place = lax.axis_index("tile")
    top = jnp.where(place > 0, 1.0, 0.0)
    bottom = jnp.where(place < lax.axis_size("tile") - 1, 1.0, 0.0)

    def relayout(source_ref, row, slot, z):
        for f in range(frames):
            pixels = source_ref[f, row : row + STRIP, :].astype(F32)
            for t in range(blocks):
                at = (f * blocks + t) * STRIP
                z_ref[z, at : at + STRIP, :] = pixels[:, t * LANES : (t + 1) * LANES]
        for g in range(2):
            a = [z_ref[z, pl.ds(4 * g + p, rows, stride=STRIP), :] for p in range(4)]
            b = [None] * 4
            for p in (0, 2):
                b[p] = jnp.where(odd_chunk, pltpu.roll(a[p + 1], 32, 1), a[p])
                b[p + 1] = jnp.where(odd_chunk, a[p + 1], pltpu.roll(a[p], LANES - 32, 1))
            for p in (0, 1):
                low = jnp.where(high_chunk, pltpu.roll(b[p + 2], 64, 1), b[p])
                high = jnp.where(high_chunk, b[p + 2], pltpu.roll(b[p], LANES - 64, 1))
                for q, value in ((p, low), (p + 2, high)):
                    x_ref[slot, q * rows : (q + 1) * rows, g * LANES : (g + 1) * LANES] = value.astype(BF16)

    def store(lo_ref, hi_ref, slot, jj, lo, hi):
        lo_ref[slot, jj * rows : (jj + 1) * rows, :] = lo.astype(BF16)
        hi_ref[slot, (jj + 1) * rows : (jj + 2) * rows, :] = hi.astype(BF16)
        if jj == 0:
            up = jnp.where(group == blocks - 1, 0.0, pltpu.roll(lo, rows - 1, 0))
            lo_ref[slot, 16 * rows : 17 * rows, :] = up.astype(BF16)
        if jj == 15:
            down = jnp.where(group == 0, 0.0, pltpu.roll(hi, 1, 0))
            hi_ref[slot, 0:rows, :] = down.astype(BF16)

    def embed(start, count, scale):
        summed = jnp.dot(
            x_ref[start : start + count].reshape(count * 4 * rows, 256),
            win_ref[...],
            preferred_element_type=F32,
        )
        bias = jnp.concatenate([patch_bias_ref[...]] * 4, axis=1)
        for s in range(count):
            for q in range(4):
                for j in range(4):
                    at = (s * 4 + q) * rows
                    part = jnp.maximum(summed[at : at + rows, j * 256 : (j + 1) * 256] + bias, 0.0)
                    if scale is not None:
                        part = part * scale
                    store(f0lo_ref, f0hi_ref, start + s, 4 * q + j, part[:, 0:LANES], part[:, LANES:])

    def gather(lo_ref, hi_ref, start, count):
        def take(ref, offset):
            return ref[start : start + count, offset : offset + m, :].reshape(count * m, LANES)

        return [take(lo_ref, 0), take(hi_ref, rows), take(hi_ref, 0), take(lo_ref, rows)]

    def conv(lo_ref, hi_ref, weights_ref, layer, count):
        first = gather(lo_ref, hi_ref, 0, count)
        second = gather(lo_ref, hi_ref, 1, count)
        summed = jnp.dot(
            jnp.concatenate(first + second, axis=1), weights_ref[...], preferred_element_type=F32
        )
        bias = jnp.concatenate([conv_bias_ref[layer : layer + 1, :]] * 4, axis=1)
        even = lane < 64
        for s in range(count):
            for jj in range(16):
                at = s * m + jj * rows
                part = jnp.maximum(summed[at : at + rows] + bias, 0.0)
                halves = []
                for c in range(2):
                    below = first[c][at : at + rows].astype(F32)
                    above = second[c][at : at + rows].astype(F32)
                    kept = jnp.where(even, above, below) if layer == 0 else jnp.where(even, below, above)
                    halves.append(kept + part[:, c * LANES : (c + 1) * LANES])
                yield s, jj, halves

    def process(count, scale, row_scale):
        embed(1, count, scale)
        for s, jj, halves in conv(f0lo_ref, f0hi_ref, w1_ref, 0, count):
            if s == 0:
                halves = [half * row_scale for half in halves]
            store(f1lo_ref, f1hi_ref, s + 1, jj, *halves)
        for s, jj, halves in conv(f1lo_ref, f1hi_ref, w2_ref, 1, count):
            q, j = jj // 4, jj % 4
            for c in range(2):
                at = j * 256 + c * LANES
                f2_ref[s, q * rows : (q + 1) * rows, at : at + LANES] = halves[c].astype(BF16)
        decoded = jnp.dot(
            f2_ref[0:count].reshape(count * 4 * rows, 1024), wd_ref[...], preferred_element_type=F32
        )
        for s in range(count):
            part = decoded[s * 4 * rows : (s + 1) * 4 * rows]
            out_ref[s] = (part + x_ref[s].astype(F32)).astype(BF16)

    @pl.when(step == 0)
    def _():
        prepare(patch_in_ref, conv_ref, patch_out_ref, win_ref, w1_ref, w2_ref, wd_ref)
        relayout(above_ref, 0, 0, 0)
        embed(0, 1, top)

    @pl.when(step > 0)
    def _():
        for ref in (f0lo_ref, f0hi_ref, f1lo_ref, f1hi_ref, x_ref):
            ref[0] = ref[strips]

    @pl.when(step < last)
    def _():
        for s in range(strips):
            relayout(movie_ref, s * STRIP, s + 1, s)
        process(strips, None, jnp.where(lane < 64, 1.0, jnp.where(step == 0, top, 1.0)))

    @pl.when(step == last)
    def _():
        relayout(below_ref, 0, 1, 0)
        process(1, bottom, jnp.where(lane < 64, bottom, 1.0))


def denoise(movie, above, below, patch_in, patch_bias, conv_weight, conv_bias, patch_out, strips):
    frames, height, width = movie.shape
    total = height // STRIP
    rows = frames * (width // LANES)
    grid = total // strips
    whole = lambda a: pl.BlockSpec(a.shape, lambda n: (0,) * a.ndim)
    flops = 2 * total * rows * 16 * (2 * 1024 * 256 + 256 * 256 + 256 * 256)
    return pl.pallas_call(
        functools.partial(denoise_kernel, strips),
        grid=(grid + 1,),
        in_specs=[
            pl.BlockSpec((frames, strips * STRIP, width), lambda n: (0, jnp.minimum(n, grid - 1), 0)),
            whole(above),
            whole(below),
            whole(patch_in),
            whole(patch_bias),
            whole(conv_weight),
            whole(conv_bias),
            whole(patch_out),
        ],
        out_specs=pl.BlockSpec((strips, 4 * rows, 256), lambda n: (n, 0, 0)),
        out_shape=jax.ShapeDtypeStruct((total + strips, 4 * rows, 256), BF16),
        scratch_shapes=[
            pltpu.VMEM((256, 1024), BF16),
            pltpu.VMEM((1024, 256), BF16),
            pltpu.VMEM((1024, 256), BF16),
            pltpu.VMEM((1024, 256), BF16),
            pltpu.VMEM((strips, rows * STRIP, LANES), F32),
            pltpu.VMEM((strips + 1, 4 * rows, 256), BF16),
        ]
        + [pltpu.VMEM((strips + 1, 17 * rows, LANES), BF16)] * 4
        + [pltpu.VMEM((strips, 4 * rows, 1024), BF16)],
        compiler_params=pltpu.CompilerParams(vmem_limit_bytes=VMEM_BYTES),
        cost_estimate=pl.CostEstimate(flops=flops, bytes_accessed=8 << 20, transcendentals=0),
        name="denoise",
    )(movie, above, below, patch_in, patch_bias, conv_weight, conv_bias, patch_out)


def cells_kernel(frames, own, denoised_ref, footprint_ref, cell_ref, window_ref, out_ref):
    rows = denoised_ref.shape[1] // 4
    blocks = rows // frames
    slots = footprint_ref.shape[1]
    n = blocks * slots
    owned = out_ref.shape[0]
    kb = pl.program_id(0)

    def flat(ref):
        return jnp.concatenate([ref[pl.ds(kb * blocks + t, 1), :] for t in range(blocks)], axis=1)

    lhs = []
    for iw in range(4):
        lhs.append(
            jnp.concatenate([denoised_ref[16 * kb + 4 * iw + i4 + 1] for i4 in range(4)], axis=1)
        )
    weights = footprint_ref[...].reshape(n, footprint_ref.shape[2])
    every = lax.dot_general(jnp.concatenate(lhs, axis=0), weights, NT, preferred_element_type=F32)
    group = lax.broadcasted_iota(jnp.int32, (blocks, n), 0)
    block_of = lax.broadcasted_iota(jnp.int32, (1, n), 1) // slots
    target = flat(window_ref) * blocks + block_of
    sums = []
    for f in range(frames):
        total = jnp.zeros((blocks, n), F32)
        for w in range(16):
            at = w * rows + f * blocks
            total = total + jnp.where(target == group + w * blocks, every[at : at + blocks, :], 0.0)
        sums.append(jnp.sum(total, axis=0, keepdims=True))
    slot_sums = jnp.concatenate(sums, axis=0)
    cell = flat(cell_ref)
    owner = jnp.floor((cell.astype(F32) + 0.5) * (1.0 / own)).astype(jnp.int32)
    low = cell - owner * own
    row_owner = lax.broadcasted_iota(jnp.int32, (owned, n), 0) // frames
    onehot = jnp.where(lax.broadcasted_iota(jnp.int32, (own, n), 0) == low, 1.0, 0.0).astype(BF16)
    spread = jnp.where(
        row_owner == owner, jnp.concatenate([slot_sums] * (owned // frames), axis=0), 0.0
    )
    acc = None
    for _ in range(3):
        piece = spread.astype(BF16)
        spread = spread - piece.astype(F32)
        part = lax.dot_general(piece, onehot, NT, preferred_element_type=F32)
        acc = part if acc is None else acc + part

    @pl.when(kb == 0)
    def _():
        out_ref[...] = acc

    @pl.when(kb > 0)
    def _():
        out_ref[...] = out_ref[...] + acc


def cells(denoised, footprint, slot_cell, window, frames, own, owners):
    padded, rows4, _ = denoised.shape
    blocks = rows4 // (4 * frames)
    count, slots, pixels = footprint.shape
    whole = lambda a: pl.BlockSpec(a.shape, lambda n: (0,) * a.ndim)
    return pl.pallas_call(
        functools.partial(cells_kernel, frames, own),
        grid=(count // blocks,),
        in_specs=[
            whole(denoised),
            pl.BlockSpec((blocks, slots, pixels), lambda n: (n, 0, 0)),
            whole(slot_cell),
            whole(window),
        ],
        out_specs=pl.BlockSpec((owners * frames, own), lambda n: (0, 0)),
        out_shape=jax.ShapeDtypeStruct((owners * frames, own), F32),
        compiler_params=pltpu.CompilerParams(vmem_limit_bytes=VMEM_BYTES),
        cost_estimate=pl.CostEstimate(flops=2 << 30, bytes_accessed=5 << 20, transcendentals=0),
        name="cells",
    )(denoised, footprint, slot_cell, window)


def spikes_kernel(tm, tile, frames, moved_ref, decay_ref, out_ref):
    own = out_ref.shape[1]
    pieces = []
    for a in range(tm):
        total = jnp.zeros((frames, own), F32)
        for b in range(tile):
            at = (a * tile + b) * frames
            total = total + moved_ref[at : at + frames, :]
        pieces.append(total)
    traces = jnp.concatenate(pieces, axis=0)
    count = tm * frames
    centered = traces - jnp.sum(traces, axis=0, keepdims=True) * (1.0 / count)
    previous = jnp.concatenate([jnp.zeros((1, own), F32), centered[:-1]], axis=0)
    spikes = centered - decay_ref[...] * previous
    power = jnp.sum(spikes * spikes, axis=0, keepdims=True) * (1.0 / count)
    out_ref[...] = spikes / jnp.sqrt(power + 1e-05)


def body(
    movie,
    patch_in,
    patch_bias,
    conv_weight,
    conv_bias,
    patch_out,
    footprint,
    slot_cell,
    slot_window_index,
    decay,
):
    frames = movie.shape[0]
    own = decay.shape[0]
    tm, tile = lax.axis_size("tm"), lax.axis_size("tile")
    forward = [(i, i + 1) for i in range(tile - 1)]
    backward = [(target, source) for source, target in forward]
    above = lax.ppermute(movie[:, -STRIP:], "tile", forward)
    below = lax.ppermute(movie[:, :STRIP], "tile", backward)
    slots = lax.all_gather(footprint, "tm", axis=1, tiled=True)
    denoised = denoise(
        movie,
        above,
        below,
        patch_in,
        patch_bias[None, :],
        conv_weight,
        conv_bias,
        patch_out,
        STRIPS if movie.shape[1] % (STRIPS * STRIP) == 0 else 2,
    )
    per_cell = cells(denoised, slots, slot_cell, slot_window_index, frames, own, tm * tile)
    moved = lax.all_to_all(per_cell, ("tm", "tile"), split_axis=0, concat_axis=0, tiled=True)
    return pl.pallas_call(
        functools.partial(spikes_kernel, tm, tile, frames),
        out_shape=jax.ShapeDtypeStruct((tm * frames, own), F32),
        name="spikes",
    )(moved, decay[None, :])


def solution(mesh):
    placed = (
        P(("field", "tm"), "tile", None),
        P(),
        P(),
        P(),
        P(),
        P(),
        P(("field", "tile"), "tm", None),
        P(("field", "tile"), None),
        P(("field", "tile"), None),
        P(("field", "tm", "tile")),
    )
    return jax.shard_map(
        body,
        mesh=mesh,
        in_specs=placed,
        out_specs=P(None, ("field", "tm", "tile")),
        check_vma=False,
    )
```

time: 105 us -> 91.8 us (0.87)
  local copies, waits for them, and re-layouts: 14.2 us -> 4.38 us
  Pallas kernels: 56.5 us -> 51.9 us
  waiting for transfers between devices: 0.74 us -> 4.19 us
  blocking collectives: 13.4 us -> 11.4 us
    unnamed x27 -> x5, local copies, waits for them, and re-layouts: 10 us -> 2 us
    pallas_call x4 -> x2, Pallas kernels: 55 us -> 50.4 us  [the longest x1 45.2 us: denoise(): pl.pallas_call(functools.partial(denoise_kernel, strips), grid=(grid + 1,...]
    ppermute x1, waiting for transfers between devices: 0.01 us -> 3.47 us  [body(): below = lax.ppermute(movie[:, :STRIP], 'tile', backward)]
    all_to_all x1, blocking collectives: 13.4 us -> 11.4 us  [body(): lax.all_to_all(per_cell, ('tm', 'tile'), split_axis=0, concat_axis=0, til...]
    another operation x4 -> x0, local copies, waits for them, and re-layouts: 1.51 us -> none  [the longest x2 0.76 us: body(): bias12 = jnp.tile(conv_bias, (1, 4))]
  transfers between devices with their start and end apart: 3 -> 3, of which waited for: 0 -> 1; matrix products, arithmetic and copies ran while one was open for 5% -> 2% of each run, Pallas kernels for 50% -> 49%
where the time goes in v2:
time: 91.8 us; the launch traced here: 91.4 us
  Pallas kernels  51.9 us (57%)
  between operations  13.4 us (15%)
  blocking collectives  11.4 us (12%)
  starting transfers between devices  6.23 us (7%)
  local copies, waits for them, and re-layouts  4.38 us (5%)
  waiting for transfers between devices  4.19 us (5%)
    pallas_call x1, Pallas kernels, denoise(): pl.pallas_call(functools.partial(denoise_kernel, strips), grid=(grid + 1,...  45.2 us
    all_to_all x1, blocking collectives, body(): lax.all_to_all(per_cell, ('tm', 'tile'), split_axis=0, concat_axis=0, til...  11.4 us
    pallas_call x1, Pallas kernels, cells(): pl.pallas_call(functools.partial(cells_kernel, frames, own), grid=(count...  5.14 us
    ppermute x1, starting transfers between devices, body(): above = lax.ppermute(movie[:, -STRIP:], 'tile', forward)  4.93 us
    ppermute x1, waiting for transfers between devices, body(): below = lax.ppermute(movie[:, :STRIP], 'tile', backward)  3.47 us
    unnamed x5, local copies, waits for them, and re-layouts  2 us
  transfers between devices with their start and end apart: 3, of which 1 were waited for; matrix products, arithmetic and copies ran while one was open for 2% of the time, Pallas kernels for 49%

profile of v2, /device:TPU:0, one launch (start us, length us, event | category | flops | bytes accessed | tf_op | source)
XLA Modules:
  0.0 91.4 jit_solution(13091274931986957928)
XLA Ops:
  6.5 0.0 all-gather.2.cloned.1.call-start
  6.5 0.7 all-gather.2.cloned.1.call-update
  7.3 0.9 fusion
  8.1 4.9 %collective-permute-start = (bf16[4,8,1024]{2,1,0:T(8,128)(2,1)S(1)}, bf16[4,8,1024]{2,1,0:T(8,128)(2,1)S(1)}, u32[]{:S(2)}, u32[]{:S(2)}) collective-permute-start(bf16[4,8,1024]{2,1,0:T(8,128)(2,1)S(1)} %get-tuple-element.6), channel_id=1, source_target_pairs={{0,1},{1,2},{2,3},{4,5},{5,6},{6,7},{8,9},{9,10},{10,11},{12,13},{... | collective-permute-start | bytes 196616 | tf_op jit(solution)/shard_map/ppermute | solution.py:372
  13.1 1.3 %collective-permute-start.1 = (bf16[4,8,1024]{2,1,0:T(8,128)(2,1)S(1)}, bf16[4,8,1024]{2,1,0:T(8,128)(2,1)S(1)}, u32[]{:S(2)}, u32[]{:S(2)}) collective-permute-start(bf16[4,8,1024]{2,1,0:T(8,128)(2,1)S(1)} %get-tuple-element.5), channel_id=1, source_target_pairs={{1,0},{2,1},{3,2},{5,4},{6,5},{7,6},{9,8},{10,9},{11,10},{13,12},{... | collective-permute-start | bytes 196616 | tf_op jit(solution)/shard_map/ppermute | solution.py:373
  14.4 1.4 %copy.11.patch_out_ref = bf16[64,16]{1,0:T(8,128)(2,1)} copy(bf16[64,16]{0,1:T(8,128)(2,1)} %param.15) | data formatting | bytes 4096 | tf_op args[5]
  15.8 0.0 collective-permute-done.above_ref
  15.8 0.0 copy-start
  15.8 3.5 %collective-permute-done.1.below_ref = bf16[4,8,1024]{2,1,0:T(8,128)(2,1)S(1)} collective-permute-done((bf16[4,8,1024]{2,1,0:T(8,128)(2,1)S(1)}, bf16[4,8,1024]{2,1,0:T(8,128)(2,1)S(1)}, u32[]{:S(2)}, u32[]{:S(2)}) %collective-permute-start.1) | collective-permute-done | bytes 65568 | tf_op jit(solution)/shard_map/ppermute | solution.py:373
  19.2 0.0 copy-start.1
  19.2 0.0 copy-done
  19.2 0.6 copy-done.1
  19.9 45.2 %denoise.1.denoised_ref = bf16[36,128,256]{2,1,0:T(8,128)(2,1)} custom-call(bf16[4,256,1024]{2,1,0:T(8,128)(2,1)} %movie_ref.1, bf16[4,8,1024]{2,1,0:T(8,128)(2,1)} %copy-done, bf16[4,8,1024]{2,1,0:T(8,128)(2,1)} %copy-done.1, bf16[16,64]{1,0:T(8,128)(2,1)} %patch_in_ref.1, f32[1,64]{1,0:T(1,128)} %bitcast.3, bf16[2,9,64,64]{3,2,1,0:T(8,128)(2,1)} %conv_ref.1, ...), custom_call_target="tpu_custom_call" | custom-call | flops 21474836480 | bytes 8388608 | tf_op jit(solution)/shard_map/denoise/pallas_call | solution.py:231
  65.1 0.0 all-gather.2.cloned.1.call-done.footprint_ref
  65.1 5.1 %cells.1 = f32[64,192]{1,0:T(8,128)} custom-call(bf16[36,128,256]{2,1,0:T(8,128)(2,1)} %denoise.1.denoised_ref, bf16[16,64,1024]{2,1,0:T(8,128)(2,1)} %all-gather.2.cloned.1.call-done.footprint_ref, s32[16,64]{1,0:T(8,128)} %cell_ref.1, s32[16,64]{1,0:T(8,128)} %window_ref.1), custom_call_target="tpu_custom_call" | custom-call | flops 2147483648 | bytes 5242880 | tf_op jit(solution)/shard_map/cells/pallas_call | solution.py:320
  70.2 0.9 all_to_all.7
  71.1 11.4 %all_to_all.11 = f32[16,4,192]{2,1,0:T(4,128)S(1)} all-to-all(f32[16,4,192]{2,1,0:T(4,128)S(1)} %all_to_all.7), channel_id=1, replica_groups=mesh['field'=2,'tm'=4,'tile'=4] {'tm','tile'}, dimensions={0} | all-to-all | bytes 98304 | tf_op jit(solution)/shard_map/all_to_all | solution.py:387
  82.5 0.6 all_to_all.9.moved_ref
  83.1 1.5 %spikes.1 = f32[16,192]{1,0:T(8,128)} custom-call(f32[64,192]{1,0:T(8,128)} %all_to_all.9.moved_ref, f32[1,192]{1,0:T(1,128)} %bitcast.2), custom_call_target="tpu_custom_call" | custom-call | tf_op jit(solution)/shard_map/spikes/pallas_call | solution.py:388
Async XLA Ops:
  6.5 58.6 %all-gather.2.cloned.1.call-start = ((), (), s32[]{:S(2)}) async-start(), calls=%async_computation.1 | async-start | bytes 2621440 | tf_op jit(solution)/shard_map/all_gather | solution.py:374
  8.1 7.6 %collective-permute-start = (bf16[4,8,1024]{2,1,0:T(8,128)(2,1)S(1)}, bf16[4,8,1024]{2,1,0:T(8,128)(2,1)S(1)}, u32[]{:S(2)}, u32[]{:S(2)}) collective-permute-start(bf16[4,8,1024]{2,1,0:T(8,128)(2,1)S(1)} %get-tuple-element.6), channel_id=1, source_target_pairs={{0,1},{1,2},{2,3},{4,5},{5,6},{6,7},{8,9},{9,10},{10,11},{12,13},{... | collective-permute-start | bytes 196616 | tf_op jit(solution)/shard_map/ppermute | solution.py:372
  13.1 6.2 %collective-permute-start.1 = (bf16[4,8,1024]{2,1,0:T(8,128)(2,1)S(1)}, bf16[4,8,1024]{2,1,0:T(8,128)(2,1)S(1)}, u32[]{:S(2)}, u32[]{:S(2)}) collective-permute-start(bf16[4,8,1024]{2,1,0:T(8,128)(2,1)S(1)} %get-tuple-element.5), channel_id=1, source_target_pairs={{1,0},{2,1},{3,2},{5,4},{6,5},{7,6},{9,8},{10,9},{11,10},{13,12},{... | collective-permute-start | bytes 196616 | tf_op jit(solution)/shard_map/ppermute | solution.py:373
  15.8 3.5 %copy-start = (bf16[4,8,1024]{2,1,0:T(8,128)(2,1)}, bf16[4,8,1024]{2,1,0:T(8,128)(2,1)S(1)}, u32[]{:S(2)}) copy-start(bf16[4,8,1024]{2,1,0:T(8,128)(2,1)S(1)} %collective-permute-done.above_ref) | copy-start | bytes 196612
  19.2 0.6 copy-start.1
Sparse Core Ops, SparseCore 0:
  8.9 25.2 all-gather.1

commit v3 on v2

--- a/solution.py
+++ b/solution.py
@@ -10,7 +10,8 @@
 BLK = 128
 LANES = 128
 STRIP = 8
-STRIPS = 4
+PAD = 3
+CHUNK = 64
 VMEM_BYTES = 60 << 20
 NT = (((1,), (1,)), ((), ()))
 F32 = jnp.float32
@@ -38,11 +39,13 @@
 
 def prepare(patch_in_ref, conv_ref, patch_out_ref, win_ref, w1_ref, w2_ref, wd_ref):
     chan = patch_in_ref.shape[1]
-    pixel = lax.broadcasted_iota(jnp.int32, (256, 16), 0)
-    tap = lax.broadcasted_iota(jnp.int32, (256, 16), 1)
-    sel = (((pixel // 32) % 4) * 4 + pixel % 4 == tap).astype(BF16)
-    spread_in = jnp.dot(sel, patch_in_ref[...], preferred_element_type=F32)
-    spread_out = lax.dot_general(patch_out_ref[...], sel, NT, preferred_element_type=F32)
+
+    def spread(taps):
+        parts = [jnp.concatenate([taps[4 * a : 4 * a + 4]] * 8, axis=0) for a in range(4)]
+        return jnp.concatenate(parts * 2, axis=0)
+
+    spread_in = spread(patch_in_ref[...].astype(F32))
+    spread_out = spread(patch_out_ref[...].astype(F32).T).T
     k = lax.broadcasted_iota(jnp.int32, (256, 2 * chan), 0)
     lane = lax.broadcasted_iota(jnp.int32, (256, 2 * chan), 1)
     wide_in = jnp.concatenate([spread_in, spread_in], axis=1)
@@ -55,16 +58,9 @@
     for pair in range(8):
         keep = ((k % 32) // 4 == pair) & (k // 128 == half)
         wd_ref[pair * 2 * chan : (pair + 1) * 2 * chan, :] = jnp.where(keep, wide_out, 0.0).astype(BF16)
-    eye = (
-        lax.broadcasted_iota(jnp.int32, (chan, chan), 0)
-        == lax.broadcasted_iota(jnp.int32, (chan, chan), 1)
-    ).astype(BF16)
     blank = jnp.zeros((chan, chan), F32)
     for layer, out in enumerate((w1_ref, w2_ref)):
-        turned = [
-            lax.dot_general(eye, conv_ref[layer, tap], NT, preferred_element_type=F32)
-            for tap in range(9)
-        ]
+        turned = [conv_ref[layer, tap].astype(F32).T for tap in range(9)]
         for row, taps in enumerate(conv_taps(layer)):
             for c in range(2):
                 pair = [blank if taps[2 * c + h] is None else turned[taps[2 * c + h]] for h in range(2)]
@@ -73,8 +69,19 @@
                 ).astype(BF16)
 
 
+def spread_jobs(units, jobs, lead=0, rate=None):
+    done = 0
+    for at, unit in enumerate(units):
+        want = lead + (at * (len(jobs) - lead) // len(units) if rate is None else at * rate)
+        while done < min(want, len(jobs)):
+            jobs[done]()
+            done += 1
+        unit()
+    for job in jobs[done:]:
+        job()
+
+
 def denoise_kernel(
-    strips,
     movie_ref,
     above_ref,
     below_ref,
@@ -88,6 +95,7 @@
     w1_ref,
     w2_ref,
     wd_ref,
+    bias_ref,
     z_ref,
     x_ref,
     f0lo_ref,
@@ -97,22 +105,25 @@
     f2_ref,
 ):
     frames = movie_ref.shape[0]
+    total = movie_ref.shape[1] // STRIP
     blocks = movie_ref.shape[2] // LANES
     rows = frames * blocks
     m = 16 * rows
+    patch_rows = 2 * 4 * rows
+    steps = total // 2 + 1
     lane = lax.broadcasted_iota(jnp.int32, (rows, LANES), 1)
     group = lax.broadcasted_iota(jnp.int32, (rows, LANES), 0) % blocks
     odd_chunk = (lane // 32) % 2 == 1
     high_chunk = lane // 64 == 1
-    step = pl.program_id(0)
-    last = pl.num_programs(0) - 1
+    even = lane < 64
     place = lax.axis_index("tile")
     top = jnp.where(place > 0, 1.0, 0.0)
     bottom = jnp.where(place < lax.axis_size("tile") - 1, 1.0, 0.0)
+    per = CHUNK // rows
 
     def relayout(source_ref, row, slot, z):
         for f in range(frames):
-            pixels = source_ref[f, row : row + STRIP, :].astype(F32)
+            pixels = source_ref[f, pl.ds(row, STRIP), :].astype(F32)
             for t in range(blocks):
                 at = (f * blocks + t) * STRIP
                 z_ref[z, at : at + STRIP, :] = pixels[:, t * LANES : (t + 1) * LANES]
@@ -138,121 +149,276 @@
             down = jnp.where(group == 0, 0.0, pltpu.roll(hi, 1, 0))
             hi_ref[slot, 0:rows, :] = down.astype(BF16)
 
-    def embed(start, count, scale):
-        summed = jnp.dot(
-            x_ref[start : start + count].reshape(count * 4 * rows, 256),
-            win_ref[...],
-            preferred_element_type=F32,
-        )
-        bias = jnp.concatenate([patch_bias_ref[...]] * 4, axis=1)
-        for s in range(count):
-            for q in range(4):
-                for j in range(4):
-                    at = (s * 4 + q) * rows
-                    part = jnp.maximum(summed[at : at + rows, j * 256 : (j + 1) * 256] + bias, 0.0)
-                    if scale is not None:
-                        part = part * scale
-                    store(f0lo_ref, f0hi_ref, start + s, 4 * q + j, part[:, 0:LANES], part[:, LANES:])
-
-    def gather(lo_ref, hi_ref, start, count):
-        def take(ref, offset):
-            return ref[start : start + count, offset : offset + m, :].reshape(count * m, LANES)
-
-        return [take(lo_ref, 0), take(hi_ref, rows), take(hi_ref, 0), take(lo_ref, rows)]
-
-    def conv(lo_ref, hi_ref, weights_ref, layer, count):
-        first = gather(lo_ref, hi_ref, 0, count)
-        second = gather(lo_ref, hi_ref, 1, count)
-        summed = jnp.dot(
-            jnp.concatenate(first + second, axis=1), weights_ref[...], preferred_element_type=F32
-        )
-        bias = jnp.concatenate([conv_bias_ref[layer : layer + 1, :]] * 4, axis=1)
-        even = lane < 64
-        for s in range(count):
-            for jj in range(16):
-                at = s * m + jj * rows
-                part = jnp.maximum(summed[at : at + rows] + bias, 0.0)
-                halves = []
-                for c in range(2):
-                    below = first[c][at : at + rows].astype(F32)
-                    above = second[c][at : at + rows].astype(F32)
-                    kept = jnp.where(even, above, below) if layer == 0 else jnp.where(even, below, above)
-                    halves.append(kept + part[:, c * LANES : (c + 1) * LANES])
-                yield s, jj, halves
-
-    def process(count, scale, row_scale):
-        embed(1, count, scale)
-        for s, jj, halves in conv(f0lo_ref, f0hi_ref, w1_ref, 0, count):
-            if s == 0:
-                halves = [half * row_scale for half in halves]
-            store(f1lo_ref, f1hi_ref, s + 1, jj, *halves)
-        for s, jj, halves in conv(f1lo_ref, f1hi_ref, w2_ref, 1, count):
+    def with_accumulators(*acc):
+        count = m // CHUNK
+        half = count // 2
+        quads = [
+            [[acc[2 * count * u + half * at + c] for c in range(half)] for u in range(2)]
+            for at in range(4)
+        ]
+
+        def joined(*at):
+            return [[ref for index in at for ref in quads[index][u]] for u in range(2)]
+
+        decode_acc = joined(0)
+        first_acc = (joined(0, 1), joined(0, 3))
+        embed_acc = (joined(2, 3), joined(2, 1))
+        second_acc = (joined(1, 2), joined(3, 2))
+
+        def products(tiles):
+            register = [0]
+
+            def push(tile):
+                for u in range(2):
+                    pltpu.matmul_push_rhs(tile[0][u](), register[0] % 2, u)
+                register[0] += 1
+
+            units = []
+            for at, tile in enumerate(tiles):
+                for c in range(len(tile[1][0])):
+
+                    def unit(at=at, tile=tile, c=c):
+                        if c == 0:
+                            if at == 0:
+                                push(tile)
+                            if at + 1 < len(tiles):
+                                push(tiles[at + 1])
+                        for u in range(2):
+                            ref, operand = tile[1][u][c]
+                            pltpu.matmul_acc_lhs(
+                                ref, operand(), load_staged_rhs=at % 2 if c == 0 else None
+                            )
+
+                    units.append(unit)
+            return units
+
+        def conv_tiles(lo_ref, hi_ref, w_ref, accs, slots):
+            tiles = []
+            for k in range(4):
+                side = k % 2
+                weight = lambda k=k: w_ref[k * 256 : (k + 1) * 256, :]
+                lists = []
+                for u in range(2):
+                    slot = slots[u + k // 2]
+                    pairs = []
+                    for c in range(count):
+
+                        def operand(slot=slot, at=c * CHUNK, side=side):
+                            if side == 0:
+                                parts = (
+                                    lo_ref[slot, at : at + CHUNK, :],
+                                    hi_ref[slot, at + rows : at + rows + CHUNK, :],
+                                )
+                            else:
+                                parts = (
+                                    hi_ref[slot, at : at + CHUNK, :],
+                                    lo_ref[slot, at + rows : at + rows + CHUNK, :],
+                                )
+                            return jnp.concatenate(parts, axis=1)
+
+                        pairs.append((accs[u][c], operand))
+                    lists.append(pairs)
+                tiles.append(((weight, weight), lists))
+            return tiles
+
+        def conv_jobs(lo_ref, hi_ref, layer, accs, slots, finish):
+            jobs = []
+            for c in range(count):
+                for u in range(2):
+
+                    def job(c=c, u=u):
+                        value = jnp.maximum(pltpu.matmul_pop(accs[u][c]) + bias_ref[layer + 1 : layer + 2, :], 0.0)
+                        for r in range(per):
+                            jj = c * per + r
+                            halves = []
+                            for h, (ref, shift) in enumerate(((lo_ref, 0), (hi_ref, rows))):
+                                at = jj * rows + shift
+                                below = ref[slots[u], at : at + rows, :].astype(F32)
+                                above = ref[slots[u + 1], at : at + rows, :].astype(F32)
+                                kept = (
+                                    jnp.where(even, above, below)
+                                    if layer == 0
+                                    else jnp.where(even, below, above)
+                                )
+                                part = value[r * rows : (r + 1) * rows, h * LANES : (h + 1) * LANES]
+                                halves.append(kept + part)
+                            finish(u, jj, halves)
+
+                    jobs.append(job)
+            return jobs
+
+        def embed_tiles(first, accs):
+            tiles = []
+            for k in range(2):
+                weights, lists = [], []
+                for u in range(2):
+                    j = 2 * u + k
+                    weights.append(lambda j=j: win_ref[:, j * 256 : (j + 1) * 256])
+                    pairs = []
+                    for c in range(patch_rows // CHUNK):
+
+                        def operand(c=c):
+                            s, at = c * CHUNK // (4 * rows), c * CHUNK % (4 * rows)
+                            return x_ref[first + s, at : at + CHUNK, :]
+
+                        pairs.append((accs[u][k * (patch_rows // CHUNK) + c], operand))
+                    lists.append(pairs)
+                tiles.append((weights, lists))
+            return tiles
+
+        def embed_jobs(slots, accs):
+            jobs = []
+            for k in range(2):
+                for c in range(patch_rows // CHUNK):
+                    for u in range(2):
+
+                        def job(k=k, c=c, u=u):
+                            j = 2 * u + k
+                            ref = accs[u][k * (patch_rows // CHUNK) + c]
+                            value = jnp.maximum(pltpu.matmul_pop(ref) + bias_ref[0:1, :], 0.0)
+                            for r in range(per):
+                                s, q = divmod(c * per + r, 4)
+                                part = value[r * rows : (r + 1) * rows]
+                                store(
+                                    f0lo_ref, f0hi_ref, slots[s], 4 * q + j, part[:, 0:LANES], part[:, LANES:]
+                                )
+
+                        jobs.append(job)
+            return jobs
+
+        def decode_tiles():
+            tiles = []
+            for k in range(2):
+                weights, lists = [], []
+                for u in range(2):
+                    tile = 2 * u + k
+                    weights.append(lambda tile=tile: wd_ref[tile * 256 : (tile + 1) * 256, :])
+                    lists.append(
+                        [
+                            (
+                                decode_acc[u][c],
+                                lambda c=c, tile=tile: f2_ref[
+                                    c * CHUNK : (c + 1) * CHUNK, tile * 256 : (tile + 1) * 256
+                                ],
+                            )
+                            for c in range(patch_rows // CHUNK)
+                        ]
+                    )
+                tiles.append((weights, lists))
+            return tiles
+
+        def decode_jobs(first):
+            jobs = []
+            for c in range(patch_rows // CHUNK):
+
+                def job(c=c):
+                    s, at = c * CHUNK // (4 * rows), c * CHUNK % (4 * rows)
+                    value = pltpu.matmul_pop(decode_acc[0][c]) + pltpu.matmul_pop(decode_acc[1][c])
+                    pixels = x_ref[first + s + PAD - 1, at : at + CHUNK, :].astype(F32)
+                    out_ref[first + s + 2, at : at + CHUNK, :] = (value + pixels).astype(BF16)
+
+                jobs.append(job)
+            return jobs
+
+        def finish_second(u, jj, halves):
             q, j = jj // 4, jj % 4
-            for c in range(2):
-                at = j * 256 + c * LANES
-                f2_ref[s, q * rows : (q + 1) * rows, at : at + LANES] = halves[c].astype(BF16)
-        decoded = jnp.dot(
-            f2_ref[0:count].reshape(count * 4 * rows, 1024), wd_ref[...], preferred_element_type=F32
-        )
-        for s in range(count):
-            part = decoded[s * 4 * rows : (s + 1) * 4 * rows]
-            out_ref[s] = (part + x_ref[s].astype(F32)).astype(BF16)
-
-    @pl.when(step == 0)
-    def _():
+            for h in range(2):
+                at = j * 256 + h * LANES
+                f2_ref[(4 * u + q) * rows : (4 * u + q + 1) * rows, at : at + LANES] = halves[h].astype(BF16)
+
+        def step(n, parity, more):
+            now = (0, 1) if parity == 0 else (2, 3)
+            nxt = (2, 3) if parity == 0 else (0, 1)
+            slots = (nxt[1],) + now
+            before = (now[1],) + nxt
+            scale = None
+            if parity == 0:
+                even_scale = jnp.where(n == steps - 1, bottom, 1.0)
+                odd_scale = jnp.where(n == 0, top, 1.0)
+                scale = jnp.where(even, even_scale, odd_scale)
+
+            def finish_first(u, jj, halves):
+                if u == 1 and scale is not None:
+                    halves = [half * scale for half in halves]
+                store(f1lo_ref, f1hi_ref, now[u], jj, *halves)
+
+            jobs = conv_jobs(f1lo_ref, f1hi_ref, 1, second_acc[1 - parity], before, finish_second)
+            if more:
+                for s in range(2):
+
+                    def job(s=s):
+                        strip = jnp.minimum(2 * n + 4, total - 2)
+                        row = pl.multiple_of(strip * STRIP, 2 * STRIP)
+                        relayout(movie_ref, row + s * STRIP, strip + 1 + s + PAD, s)
+
+                    jobs.append(job)
+            accs = first_acc[parity]
+            spread_jobs(products(conv_tiles(f0lo_ref, f0hi_ref, w1_ref, accs, slots)), jobs)
+            tiles = (embed_tiles(2 * n + 2 + PAD, embed_acc[parity]) if more else []) + decode_tiles()
+            jobs = conv_jobs(f0lo_ref, f0hi_ref, 0, accs, slots, finish_first)
+            spread_jobs(products(tiles), jobs, 0 if more else count)
+            jobs = (embed_jobs(nxt, embed_acc[parity]) if more else []) + decode_jobs(2 * n - 2)
+            accs = second_acc[parity]
+            spread_jobs(products(conv_tiles(f1lo_ref, f1hi_ref, w2_ref, accs, slots)), jobs, 0, 2)
+
+        for ref in acc:
+            pltpu.matmul_pop(ref)
         prepare(patch_in_ref, conv_ref, patch_out_ref, win_ref, w1_ref, w2_ref, wd_ref)
-        relayout(above_ref, 0, 0, 0)
-        embed(0, 1, top)
-
-    @pl.when(step > 0)
-    def _():
-        for ref in (f0lo_ref, f0hi_ref, f1lo_ref, f1hi_ref, x_ref):
-            ref[0] = ref[strips]
-
-    @pl.when(step < last)
-    def _():
-        for s in range(strips):
-            relayout(movie_ref, s * STRIP, s + 1, s)
-        process(strips, None, jnp.where(lane < 64, 1.0, jnp.where(step == 0, top, 1.0)))
-
-    @pl.when(step == last)
-    def _():
-        relayout(below_ref, 0, 1, 0)
-        process(1, bottom, jnp.where(lane < 64, bottom, 1.0))
-
-
-def denoise(movie, above, below, patch_in, patch_bias, conv_weight, conv_bias, patch_out, strips):
+        bias_ref[0:1, :] = jnp.concatenate([patch_bias_ref[...]] * 4, axis=1)
+        for layer in range(2):
+            bias_ref[layer + 1 : layer + 2, :] = jnp.concatenate(
+                [conv_bias_ref[layer : layer + 1, :]] * 4, axis=1
+            )
+        relayout(above_ref, 0, PAD, 0)
+        relayout(below_ref, 0, total + 1 + PAD, 1)
+        for strip in range(4):
+            relayout(movie_ref, strip * STRIP, strip + 1 + PAD, strip % 2)
+        spread_jobs(products(embed_tiles(PAD, embed_acc[0])), [])
+        for job in embed_jobs((0, 1), embed_acc[0]):
+            job()
+        for ref in (f0lo_ref, f0hi_ref):
+            ref[0] = (ref[0].astype(F32) * top).astype(BF16)
+
+        def pair(i, carry):
+            step(2 * i, 0, True)
+            step(2 * i + 1, 1, True)
+            return carry
+
+        lax.fori_loop(0, (steps - 1) // 2, pair, 0)
+        for ref in (f0lo_ref, f0hi_ref):
+            ref[1] = (ref[1].astype(F32) * bottom).astype(BF16)
+        step(steps - 1, 0, False)
+        for job in conv_jobs(f1lo_ref, f1hi_ref, 1, second_acc[0], (3, 0, 1), finish_second):
+            job()
+        spread_jobs(products(decode_tiles()), [])
+        for job in decode_jobs(2 * steps - 2):
+            job()
+
+    pl.run_scoped(
+        with_accumulators,
+        *[pltpu.ACC(u)((CHUNK, 256), F32) for u in range(2) for _ in range(2 * m // CHUNK)],
+    )
+
+
+def denoise(movie, above, below, patch_in, patch_bias, conv_weight, conv_bias, patch_out):
     frames, height, width = movie.shape
     total = height // STRIP
     rows = frames * (width // LANES)
-    grid = total // strips
-    whole = lambda a: pl.BlockSpec(a.shape, lambda n: (0,) * a.ndim)
     flops = 2 * total * rows * 16 * (2 * 1024 * 256 + 256 * 256 + 256 * 256)
     return pl.pallas_call(
-        functools.partial(denoise_kernel, strips),
-        grid=(grid + 1,),
-        in_specs=[
-            pl.BlockSpec((frames, strips * STRIP, width), lambda n: (0, jnp.minimum(n, grid - 1), 0)),
-            whole(above),
-            whole(below),
-            whole(patch_in),
-            whole(patch_bias),
-            whole(conv_weight),
-            whole(conv_bias),
-            whole(patch_out),
-        ],
-        out_specs=pl.BlockSpec((strips, 4 * rows, 256), lambda n: (n, 0, 0)),
-        out_shape=jax.ShapeDtypeStruct((total + strips, 4 * rows, 256), BF16),
+        denoise_kernel,
+        out_shape=jax.ShapeDtypeStruct((total + 4, 4 * rows, 256), BF16),
         scratch_shapes=[
             pltpu.VMEM((256, 1024), BF16),
             pltpu.VMEM((1024, 256), BF16),
             pltpu.VMEM((1024, 256), BF16),
             pltpu.VMEM((1024, 256), BF16),
-            pltpu.VMEM((strips, rows * STRIP, LANES), F32),
-            pltpu.VMEM((strips + 1, 4 * rows, 256), BF16),
+            pltpu.VMEM((8, 256), F32),
+            pltpu.VMEM((2, rows * STRIP, LANES), F32),
+            pltpu.VMEM((total + 2 + PAD, 4 * rows, 256), BF16),
         ]
-        + [pltpu.VMEM((strips + 1, 17 * rows, LANES), BF16)] * 4
-        + [pltpu.VMEM((strips, 4 * rows, 1024), BF16)],
+        + [pltpu.VMEM((4, 17 * rows, LANES), BF16)] * 4
+        + [pltpu.VMEM((2 * 4 * rows, 1024), BF16)],
         compiler_params=pltpu.CompilerParams(vmem_limit_bytes=VMEM_BYTES),
         cost_estimate=pl.CostEstimate(flops=flops, bytes_accessed=8 << 20, transcendentals=0),
         name="denoise",
@@ -273,7 +439,7 @@
     lhs = []
     for iw in range(4):
         lhs.append(
-            jnp.concatenate([denoised_ref[16 * kb + 4 * iw + i4 + 1] for i4 in range(4)], axis=1)
+            jnp.concatenate([denoised_ref[16 * kb + 4 * iw + i4 + 4] for i4 in range(4)], axis=1)
         )
     weights = footprint_ref[...].reshape(n, footprint_ref.shape[2])
     every = lax.dot_general(jnp.concatenate(lhs, axis=0), weights, NT, preferred_element_type=F32)
@@ -381,7 +547,6 @@
         conv_weight,
         conv_bias,
         patch_out,
-        STRIPS if movie.shape[1] % (STRIPS * STRIP) == 0 else 2,
     )
     per_cell = cells(denoised, slots, slot_cell, slot_window_index, frames, own, tm * tile)
     moved = lax.all_to_all(per_cell, ("tm", "tile"), split_axis=0, concat_axis=0, tiled=True)

time: 91.8 us -> 80.9 us (0.88)
  Pallas kernels: 51.9 us -> 41 us
    pallas_call x1, Pallas kernels: 45.2 us -> 34.3 us  [denoise(): pl.pallas_call(denoise_kernel, out_shape=jax.ShapeDtypeStruct((total + 4,...]
  transfers between devices with their start and end apart: 3 -> 3, of which waited for: 1 -> 1; matrix products, arithmetic and copies ran while one was open for 2% -> 3% of each run, Pallas kernels for 49% -> 43%
where the time goes in v3:
time: 80.9 us; the launch traced here: 80.6 us
  Pallas kernels  41 us (51%)
  between operations  13.4 us (17%)
  blocking collectives  11.4 us (14%)
  starting transfers between devices  6.23 us (8%)
  local copies, waits for them, and re-layouts  4.38 us (5%)
  waiting for transfers between devices  4.19 us (5%)
    pallas_call x1, Pallas kernels, denoise(): pl.pallas_call(denoise_kernel, out_shape=jax.ShapeDtypeStruct((total + 4,...  34.3 us
    all_to_all x1, blocking collectives, body(): lax.all_to_all(per_cell, ('tm', 'tile'), split_axis=0, concat_axis=0, til...  11.4 us
    pallas_call x1, Pallas kernels, cells(): pl.pallas_call(functools.partial(cells_kernel, frames, own), grid=(count...  5.14 us
    ppermute x1, starting transfers between devices, body(): above = lax.ppermute(movie[:, -STRIP:], 'tile', forward)  4.93 us
    ppermute x1, waiting for transfers between devices, body(): below = lax.ppermute(movie[:, :STRIP], 'tile', backward)  3.47 us
    unnamed x5, local copies, waits for them, and re-layouts  2 us
  transfers between devices with their start and end apart: 3, of which 1 were waited for; matrix products, arithmetic and copies ran while one was open for 3% of the time, Pallas kernels for 43%

profile of v3, /device:TPU:0, one launch (start us, length us, event | category | flops | bytes accessed | tf_op | source)
XLA Modules:
  0.0 80.6 jit_solution(13916886138207775216)
XLA Ops:
  6.5 0.0 all-gather.2.cloned.1.call-start
  6.5 0.7 all-gather.2.cloned.1.call-update
  7.3 0.9 %fusion = (bf16[4,8,1024]{2,1,0:T(8,128)(2,1)S(1)}, bf16[4,8,1024]{2,1,0:T(8,128)(2,1)S(1)}) fusion(bf16[4,256,1024]{2,1,0:T(8,128)(2,1)} %movie_ref.1), kind=kLoop, calls=%fused_computation | loop fusion | bytes 262144 | tf_op jit(solution)/shard_map/slice | solution.py:539
  8.1 4.9 %collective-permute-start = (bf16[4,8,1024]{2,1,0:T(8,128)(2,1)S(1)}, bf16[4,8,1024]{2,1,0:T(8,128)(2,1)S(1)}, u32[]{:S(2)}, u32[]{:S(2)}) collective-permute-start(bf16[4,8,1024]{2,1,0:T(8,128)(2,1)S(1)} %get-tuple-element.6), channel_id=1, source_target_pairs={{0,1},{1,2},{2,3},{4,5},{5,6},{6,7},{8,9},{9,10},{10,11},{12,13},{... | collective-permute-start | bytes 196616 | tf_op jit(solution)/shard_map/ppermute | solution.py:538
  13.1 1.3 %collective-permute-start.1 = (bf16[4,8,1024]{2,1,0:T(8,128)(2,1)S(1)}, bf16[4,8,1024]{2,1,0:T(8,128)(2,1)S(1)}, u32[]{:S(2)}, u32[]{:S(2)}) collective-permute-start(bf16[4,8,1024]{2,1,0:T(8,128)(2,1)S(1)} %get-tuple-element.5), channel_id=1, source_target_pairs={{1,0},{2,1},{3,2},{5,4},{6,5},{7,6},{9,8},{10,9},{11,10},{13,12},{... | collective-permute-start | bytes 196616 | tf_op jit(solution)/shard_map/ppermute | solution.py:539
  14.4 1.4 %copy.11.patch_out_ref = bf16[64,16]{1,0:T(8,128)(2,1)} copy(bf16[64,16]{0,1:T(8,128)(2,1)} %param.15) | data formatting | bytes 4096 | tf_op args[5]
  15.8 0.0 collective-permute-done.above_ref
  15.8 0.0 copy-start
  15.8 3.5 %collective-permute-done.1.below_ref = bf16[4,8,1024]{2,1,0:T(8,128)(2,1)S(1)} collective-permute-done((bf16[4,8,1024]{2,1,0:T(8,128)(2,1)S(1)}, bf16[4,8,1024]{2,1,0:T(8,128)(2,1)S(1)}, u32[]{:S(2)}, u32[]{:S(2)}) %collective-permute-start.1) | collective-permute-done | bytes 65568 | tf_op jit(solution)/shard_map/ppermute | solution.py:539
  19.2 0.0 copy-start.1
  19.2 0.0 copy-done
  19.2 0.6 copy-done.1
  19.9 34.3 %denoise.1.denoised_ref = bf16[36,128,256]{2,1,0:T(8,128)(2,1)} custom-call(bf16[4,256,1024]{2,1,0:T(8,128)(2,1)} %movie_ref.1, bf16[4,8,1024]{2,1,0:T(8,128)(2,1)} %copy-done, bf16[4,8,1024]{2,1,0:T(8,128)(2,1)} %copy-done.1, bf16[16,64]{1,0:T(8,128)(2,1)} %patch_in_ref.1, f32[1,64]{1,0:T(1,128)} %bitcast.3, bf16[2,9,64,64]{3,2,1,0:T(8,128)(2,1)} %conv_ref.1, ...), custom_call_target="tpu_custom_call" | custom-call | flops 21474836480 | bytes 8388608 | tf_op jit(solution)/shard_map/denoise/pallas_call | solution.py:408
  54.2 0.0 all-gather.2.cloned.1.call-done.footprint_ref
  54.2 5.1 %cells.1 = f32[64,192]{1,0:T(8,128)} custom-call(bf16[36,128,256]{2,1,0:T(8,128)(2,1)} %denoise.1.denoised_ref, bf16[16,64,1024]{2,1,0:T(8,128)(2,1)} %all-gather.2.cloned.1.call-done.footprint_ref, s32[16,64]{1,0:T(8,128)} %cell_ref.1, s32[16,64]{1,0:T(8,128)} %window_ref.1), custom_call_target="tpu_custom_call" | custom-call | flops 2147483648 | bytes 5242880 | tf_op jit(solution)/shard_map/cells/pallas_call | solution.py:486
  59.3 0.9 %all_to_all.7 = f32[16,4,192]{2,1,0:T(4,128)S(1)} reshape(f32[64,192]{1,0:T(8,128)} %cells.1) | data formatting | bytes 98304 | tf_op jit(solution)/shard_map/all_to_all | solution.py:552
  60.2 11.4 %all_to_all.11 = f32[16,4,192]{2,1,0:T(4,128)S(1)} all-to-all(f32[16,4,192]{2,1,0:T(4,128)S(1)} %all_to_all.7), channel_id=1, replica_groups=mesh['field'=2,'tm'=4,'tile'=4] {'tm','tile'}, dimensions={0} | all-to-all | bytes 98304 | tf_op jit(solution)/shard_map/all_to_all | solution.py:552
  71.6 0.6 all_to_all.9.moved_ref
  72.2 1.5 %spikes.1 = f32[16,192]{1,0:T(8,128)} custom-call(f32[64,192]{1,0:T(8,128)} %all_to_all.9.moved_ref, f32[1,192]{1,0:T(1,128)} %bitcast.2), custom_call_target="tpu_custom_call" | custom-call | tf_op jit(solution)/shard_map/spikes/pallas_call | solution.py:553
Async XLA Ops:
  6.5 47.7 %all-gather.2.cloned.1.call-start = ((), (), s32[]{:S(2)}) async-start(), calls=%async_computation.1 | async-start | bytes 2621440 | tf_op jit(solution)/shard_map/all_gather | solution.py:540
  8.1 7.6 %collective-permute-start = (bf16[4,8,1024]{2,1,0:T(8,128)(2,1)S(1)}, bf16[4,8,1024]{2,1,0:T(8,128)(2,1)S(1)}, u32[]{:S(2)}, u32[]{:S(2)}) collective-permute-start(bf16[4,8,1024]{2,1,0:T(8,128)(2,1)S(1)} %get-tuple-element.6), channel_id=1, source_target_pairs={{0,1},{1,2},{2,3},{4,5},{5,6},{6,7},{8,9},{9,10},{10,11},{12,13},{... | collective-permute-start | bytes 196616 | tf_op jit(solution)/shard_map/ppermute | solution.py:538
  13.1 6.2 %collective-permute-start.1 = (bf16[4,8,1024]{2,1,0:T(8,128)(2,1)S(1)}, bf16[4,8,1024]{2,1,0:T(8,128)(2,1)S(1)}, u32[]{:S(2)}, u32[]{:S(2)}) collective-permute-start(bf16[4,8,1024]{2,1,0:T(8,128)(2,1)S(1)} %get-tuple-element.5), channel_id=1, source_target_pairs={{1,0},{2,1},{3,2},{5,4},{6,5},{7,6},{9,8},{10,9},{11,10},{13,12},{... | collective-permute-start | bytes 196616 | tf_op jit(solution)/shard_map/ppermute | solution.py:539
  15.8 3.5 %copy-start = (bf16[4,8,1024]{2,1,0:T(8,128)(2,1)}, bf16[4,8,1024]{2,1,0:T(8,128)(2,1)S(1)}, u32[]{:S(2)}) copy-start(bf16[4,8,1024]{2,1,0:T(8,128)(2,1)S(1)} %collective-permute-done.above_ref) | copy-start | bytes 196612
  19.2 0.6 copy-start.1
Sparse Core Ops, SparseCore 0:
  8.9 25.2 all-gather.1

commit v4 on v3

--- a/solution.py
+++ b/solution.py
@@ -425,79 +425,96 @@
     )(movie, above, below, patch_in, patch_bias, conv_weight, conv_bias, patch_out)
 
 
-def cells_kernel(frames, own, denoised_ref, footprint_ref, cell_ref, window_ref, out_ref):
+def cells_kernel(frames, own, denoised_ref, cell_ref, window_ref, *refs):
+    pieces = refs[:-5]
+    out_ref, image_ref, weights_ref, image_sem, piece_sem = refs[-5:]
+    total = denoised_ref.shape[0] - 4
     rows = denoised_ref.shape[1] // 4
     blocks = rows // frames
-    slots = footprint_ref.shape[1]
+    share = pieces[0].shape[1]
+    slots = share * len(pieces)
     n = blocks * slots
-    owned = out_ref.shape[0]
-    kb = pl.program_id(0)
-
-    def flat(ref):
-        return jnp.concatenate([ref[pl.ds(kb * blocks + t, 1), :] for t in range(blocks)], axis=1)
-
-    lhs = []
-    for iw in range(4):
-        lhs.append(
-            jnp.concatenate([denoised_ref[16 * kb + 4 * iw + i4 + 4] for i4 in range(4)], axis=1)
+    owners = out_ref.shape[0]
+    place = lax.axis_index("tm")
+
+    def copies(kb):
+        strips, squares = pl.ds(16 * kb, 16), pl.ds(kb * blocks, blocks)
+        yield pltpu.make_async_copy(
+            denoised_ref.at[pl.ds(16 * kb + 4, 16)], image_ref.at[strips], image_sem.at[kb]
         )
-    weights = footprint_ref[...].reshape(n, footprint_ref.shape[2])
-    every = lax.dot_general(jnp.concatenate(lhs, axis=0), weights, NT, preferred_element_type=F32)
+        for at, piece in enumerate(pieces):
+            first = pl.multiple_of(lax.rem(place + at, len(pieces)) * share, share)
+            yield pltpu.make_async_copy(
+                piece.at[squares], weights_ref.at[squares, pl.ds(first, share)], piece_sem.at[kb, at]
+            )
+
+    for kb in range(total // 16):
+        for copy in copies(kb):
+            copy.start()
+
     group = lax.broadcasted_iota(jnp.int32, (blocks, n), 0)
     block_of = lax.broadcasted_iota(jnp.int32, (1, n), 1) // slots
-    target = flat(window_ref) * blocks + block_of
-    sums = []
-    for f in range(frames):
-        total = jnp.zeros((blocks, n), F32)
-        for w in range(16):
-            at = w * rows + f * blocks
-            total = total + jnp.where(target == group + w * blocks, every[at : at + blocks, :], 0.0)
-        sums.append(jnp.sum(total, axis=0, keepdims=True))
-    slot_sums = jnp.concatenate(sums, axis=0)
-    cell = flat(cell_ref)
-    owner = jnp.floor((cell.astype(F32) + 0.5) * (1.0 / own)).astype(jnp.int32)
-    low = cell - owner * own
-    row_owner = lax.broadcasted_iota(jnp.int32, (owned, n), 0) // frames
-    onehot = jnp.where(lax.broadcasted_iota(jnp.int32, (own, n), 0) == low, 1.0, 0.0).astype(BF16)
-    spread = jnp.where(
-        row_owner == owner, jnp.concatenate([slot_sums] * (owned // frames), axis=0), 0.0
-    )
+    row_owner = lax.broadcasted_iota(jnp.int32, (owners * frames, n), 0) // frames
     acc = None
-    for _ in range(3):
-        piece = spread.astype(BF16)
-        spread = spread - piece.astype(F32)
-        part = lax.dot_general(piece, onehot, NT, preferred_element_type=F32)
-        acc = part if acc is None else acc + part
-
-    @pl.when(kb == 0)
-    def _():
-        out_ref[...] = acc
-
-    @pl.when(kb > 0)
-    def _():
-        out_ref[...] = out_ref[...] + acc
-
-
-def cells(denoised, footprint, slot_cell, window, frames, own, owners):
+    for kb in range(total // 16):
+
+        def flat(ref):
+            return jnp.concatenate([ref[kb * blocks + t : kb * blocks + t + 1, :] for t in range(blocks)], axis=1)
+
+        target = flat(window_ref) * blocks + block_of
+        cell = flat(cell_ref)
+        owner = jnp.floor((cell.astype(F32) + 0.5) * (1.0 / own)).astype(jnp.int32)
+        low = cell - owner * own
+        onehot = jnp.where(lax.broadcasted_iota(jnp.int32, (own, n), 0) == low, 1.0, 0.0).astype(BF16)
+        for copy in copies(kb):
+            copy.wait()
+        lhs = []
+        for iw in range(4):
+            lhs.append(
+                jnp.concatenate([image_ref[16 * kb + 4 * iw + i4] for i4 in range(4)], axis=1)
+            )
+        weights = weights_ref[kb * blocks : (kb + 1) * blocks].reshape(n, weights_ref.shape[2])
+        every = lax.dot_general(jnp.concatenate(lhs, axis=0), weights, NT, preferred_element_type=F32)
+        sums = []
+        for f in range(frames):
+            picked = jnp.zeros((blocks, n), F32)
+            for w in range(16):
+                at = w * rows + f * blocks
+                picked = picked + jnp.where(
+                    target == group + w * blocks, every[at : at + blocks, :], 0.0
+                )
+            sums.append(jnp.sum(picked, axis=0, keepdims=True))
+        slot_sums = jnp.concatenate(sums, axis=0)
+        spread = jnp.where(row_owner == owner, jnp.concatenate([slot_sums] * owners, axis=0), 0.0)
+        for _ in range(3):
+            piece = spread.astype(BF16)
+            spread = spread - piece.astype(F32)
+            part = lax.dot_general(piece, onehot, NT, preferred_element_type=F32)
+            acc = part if acc is None else acc + part
+    for o in range(owners):
+        out_ref[o] = acc[o * frames : (o + 1) * frames]
+
+
+def cells(denoised, pieces, slot_cell, window, frames, own, owners):
     padded, rows4, _ = denoised.shape
-    blocks = rows4 // (4 * frames)
-    count, slots, pixels = footprint.shape
-    whole = lambda a: pl.BlockSpec(a.shape, lambda n: (0,) * a.ndim)
+    count, share, pixels = pieces[0].shape
+    steps = (padded - 4) // 16
+    away = pl.BlockSpec(memory_space=pl.ANY)
+    here = pl.BlockSpec(memory_space=pltpu.VMEM)
     return pl.pallas_call(
         functools.partial(cells_kernel, frames, own),
-        grid=(count // blocks,),
-        in_specs=[
-            whole(denoised),
-            pl.BlockSpec((blocks, slots, pixels), lambda n: (n, 0, 0)),
-            whole(slot_cell),
-            whole(window),
+        in_specs=[away, here, here] + [away] * len(pieces),
+        out_shape=jax.ShapeDtypeStruct((owners, frames, own), F32),
+        scratch_shapes=[
+            pltpu.VMEM((padded - 4, rows4, 256), BF16),
+            pltpu.VMEM((count, share * len(pieces), pixels), BF16),
+            pltpu.SemaphoreType.DMA((steps,)),
+            pltpu.SemaphoreType.DMA((steps, len(pieces))),
         ],
-        out_specs=pl.BlockSpec((owners * frames, own), lambda n: (0, 0)),
-        out_shape=jax.ShapeDtypeStruct((owners * frames, own), F32),
         compiler_params=pltpu.CompilerParams(vmem_limit_bytes=VMEM_BYTES),
         cost_estimate=pl.CostEstimate(flops=2 << 30, bytes_accessed=5 << 20, transcendentals=0),
         name="cells",
-    )(denoised, footprint, slot_cell, window)
+    )(denoised, slot_cell, window, *pieces)
 
 
 def spikes_kernel(tm, tile, frames, moved_ref, decay_ref, out_ref):
@@ -506,8 +523,7 @@
     for a in range(tm):
         total = jnp.zeros((frames, own), F32)
         for b in range(tile):
-            at = (a * tile + b) * frames
-            total = total + moved_ref[at : at + frames, :]
+            total = total + moved_ref[a * tile + b]
         pieces.append(total)
     traces = jnp.concatenate(pieces, axis=0)
     count = tm * frames
@@ -537,7 +553,10 @@
     backward = [(target, source) for source, target in forward]
     above = lax.ppermute(movie[:, -STRIP:], "tile", forward)
     below = lax.ppermute(movie[:, :STRIP], "tile", backward)
-    slots = lax.all_gather(footprint, "tm", axis=1, tiled=True)
+    pieces = [footprint]
+    for ahead in range(1, tm):
+        ring = [(source, (source - ahead) % tm) for source in range(tm)]
+        pieces.append(lax.ppermute(footprint, "tm", ring))
     denoised = denoise(
         movie,
         above,
@@ -548,7 +567,7 @@
         conv_bias,
         patch_out,
     )
-    per_cell = cells(denoised, slots, slot_cell, slot_window_index, frames, own, tm * tile)
+    per_cell = cells(denoised, pieces, slot_cell, slot_window_index, frames, own, tm * tile)
     moved = lax.all_to_all(per_cell, ("tm", "tile"), split_axis=0, concat_axis=0, tiled=True)
     return pl.pallas_call(
         functools.partial(spikes_kernel, tm, tile, frames),

time: 80.9 us -> 68.5 us (0.85)
  between operations: 13.4 us -> 0.06 us
  waiting for transfers between devices: 4.19 us -> 1.67 us
  starting transfers between devices: 6.23 us -> 8.04 us
    ppermute x0 -> x3, starting transfers between devices: none -> 1.82 us  [body(): pieces.append(lax.ppermute(footprint, 'tm', ring))]
    ppermute x1, waiting for transfers between devices: 3.47 us -> 1.66 us  [body(): below = lax.ppermute(movie[:, :STRIP], 'tile', backward)]
    unnamed x5 -> x11, local copies, waits for them, and re-layouts: 2 us -> 3.75 us
    all_to_all x2 -> x0, local copies, waits for them, and re-layouts: 1.5 us -> none  [body(): lax.all_to_all(per_cell, ('tm', 'tile'), split_axis=0, concat_axis=0, til...]
    all_to_all x1, blocking collectives: 11.4 us -> 12.2 us  [body(): lax.all_to_all(per_cell, ('tm', 'tile'), split_axis=0, concat_axis=0, til...]
  transfers between devices with their start and end apart: 3 -> 5, of which waited for: 1 -> 1; matrix products, arithmetic and copies ran while one was open for 3% -> 2% of each run, Pallas kernels for 43% -> 50%
where the time goes in v4:
time: 68.5 us; the launch traced here: 68.1 us
  Pallas kernels  41.5 us (61%)
  blocking collectives  12.2 us (18%)
  starting transfers between devices  8.04 us (12%)
  local copies, waits for them, and re-layouts  4.63 us (7%)
  waiting for transfers between devices  1.67 us (2%)
    pallas_call x1, Pallas kernels, denoise(): pl.pallas_call(denoise_kernel, out_shape=jax.ShapeDtypeStruct((total + 4,...  34.3 us
    all_to_all x1, blocking collectives, body(): lax.all_to_all(per_cell, ('tm', 'tile'), split_axis=0, concat_axis=0, til...  12.2 us
    pallas_call x1, Pallas kernels, cells(): pl.pallas_call(functools.partial(cells_kernel, frames, own), in_specs=[aw...  5.66 us
    ppermute x1, starting transfers between devices, body(): above = lax.ppermute(movie[:, -STRIP:], 'tile', forward)  4.93 us
    unnamed x11, local copies, waits for them, and re-layouts  3.75 us
    ppermute x3, starting transfers between devices, body(): pieces.append(lax.ppermute(footprint, 'tm', ring))  1.82 us
    ppermute x1, waiting for transfers between devices, body(): below = lax.ppermute(movie[:, :STRIP], 'tile', backward)  1.66 us
    pallas_call x1, Pallas kernels, body(): pl.pallas_call(functools.partial(spikes_kernel, tm, tile, frames), out_sh...  1.49 us
  transfers between devices with their start and end apart: 5, of which 1 were waited for; matrix products, arithmetic and copies ran while one was open for 2% of the time, Pallas kernels for 50%

profile of v4, /device:TPU:0, one launch (start us, length us, event | category | flops | bytes accessed | tf_op | source)
XLA Modules:
  0.0 68.1 jit_solution(14611855588577587801)
XLA Ops:
  0.0 0.9 %fusion = (bf16[4,8,1024]{2,1,0:T(8,128)(2,1)S(1)}, bf16[4,8,1024]{2,1,0:T(8,128)(2,1)S(1)}) fusion(bf16[4,256,1024]{2,1,0:T(8,128)(2,1)} %movie_ref.1), kind=kLoop, calls=%fused_computation | loop fusion | bytes 262144 | tf_op jit(solution)/shard_map/slice | solution.py:555
  0.9 4.9 %collective-permute-start = (bf16[4,8,1024]{2,1,0:T(8,128)(2,1)S(1)}, bf16[4,8,1024]{2,1,0:T(8,128)(2,1)S(1)}, u32[]{:S(2)}, u32[]{:S(2)}) collective-permute-start(bf16[4,8,1024]{2,1,0:T(8,128)(2,1)S(1)} %get-tuple-element.6), channel_id=1, source_target_pairs={{0,1},{1,2},{2,3},{4,5},{5,6},{6,7},{8,9},{9,10},{10,11},{12,13},{... | collective-permute-start | bytes 196616 | tf_op jit(solution)/shard_map/ppermute | solution.py:554
  5.8 1.3 %collective-permute-start.1 = (bf16[4,8,1024]{2,1,0:T(8,128)(2,1)S(1)}, bf16[4,8,1024]{2,1,0:T(8,128)(2,1)S(1)}, u32[]{:S(2)}, u32[]{:S(2)}) collective-permute-start(bf16[4,8,1024]{2,1,0:T(8,128)(2,1)S(1)} %get-tuple-element.5), channel_id=1, source_target_pairs={{1,0},{2,1},{3,2},{5,4},{6,5},{7,6},{9,8},{10,9},{11,10},{13,12},{... | collective-permute-start | bytes 196616 | tf_op jit(solution)/shard_map/ppermute | solution.py:555
  7.1 0.7 %collective-permute-start.2 = (bf16[16,16,1024]{2,1,0:T(8,128)(2,1)}, bf16[16,16,1024]{2,1,0:T(8,128)(2,1)S(1)}, u32[]{:S(2)}, u32[]{:S(2)}) collective-permute-start(bf16[16,16,1024]{2,1,0:T(8,128)(2,1)} %refs_0_.1), channel_id=1, source_target_pairs={{0,12},{4,0},{8,4},{12,8},{1,13},{5,1},{9,5},{13,9},{2,14},{6,2},{... | collective-permute-start | bytes 1572872 | tf_op jit(solution)/shard_map/ppermute | solution.py:559
  7.9 0.9 %collective-permute-start.3 = (bf16[16,16,1024]{2,1,0:T(8,128)(2,1)}, bf16[16,16,1024]{2,1,0:T(8,128)(2,1)S(1)}, u32[]{:S(2)}, u32[]{:S(2)}) collective-permute-start(bf16[16,16,1024]{2,1,0:T(8,128)(2,1)} %refs_0_.1), channel_id=1, source_target_pairs={{0,8},{4,12},{8,0},{12,4},{1,9},{5,13},{9,1},{13,5},{2,10},{6,14},... | collective-permute-start | bytes 1572872 | tf_op jit(solution)/shard_map/ppermute | solution.py:559
  8.8 0.2 collective-permute-start.4
  8.9 1.4 %copy.11.patch_out_ref = bf16[64,16]{1,0:T(8,128)(2,1)} copy(bf16[64,16]{0,1:T(8,128)(2,1)} %param.15) | data formatting | bytes 4096 | tf_op args[5]
  10.3 0.0 collective-permute-done.above_ref
  10.3 0.0 copy-start.3
  10.3 1.7 %collective-permute-done.1.below_ref = bf16[4,8,1024]{2,1,0:T(8,128)(2,1)S(1)} collective-permute-done((bf16[4,8,1024]{2,1,0:T(8,128)(2,1)S(1)}, bf16[4,8,1024]{2,1,0:T(8,128)(2,1)S(1)}, u32[]{:S(2)}, u32[]{:S(2)}) %collective-permute-start.1) | collective-permute-done | bytes 65568 | tf_op jit(solution)/shard_map/ppermute | solution.py:555
  12.0 0.0 copy-start.4
  12.0 0.0 copy-done.3
  12.0 0.6 copy-done.4
  12.6 34.3 %denoise.1.denoised_ref = bf16[36,128,256]{2,1,0:T(8,128)(2,1)} custom-call(bf16[4,256,1024]{2,1,0:T(8,128)(2,1)} %movie_ref.1, bf16[4,8,1024]{2,1,0:T(8,128)(2,1)} %copy-done.3, bf16[4,8,1024]{2,1,0:T(8,128)(2,1)} %copy-done.4, bf16[16,64]{1,0:T(8,128)(2,1)} %patch_in_ref.1, f32[1,64]{1,0:T(1,128)} %bitcast.3, bf16[2,9,64,64]{3,2,1,0:T(8,128)(2,1)} %conv_ref.1, ...), custom_call_target="tpu_custom_call" | custom-call | flops 21474836480 | bytes 8388608 | tf_op jit(solution)/shard_map/denoise/pallas_call | solution.py:408
  46.9 0.0 collective-permute-done.2.refs_1_
  47.0 0.0 copy-start
  47.0 0.0 collective-permute-done.3.refs_2_
  47.0 0.0 copy-start.1
  47.0 0.0 collective-permute-done.4.refs_3_
  47.0 0.8 %copy-done = bf16[16,16,1024]{2,1,0:T(8,128)(2,1)} copy-done((bf16[16,16,1024]{2,1,0:T(8,128)(2,1)}, bf16[16,16,1024]{2,1,0:T(8,128)(2,1)S(1)}, u32[]{:S(2)}) %copy-start) | copy-done | bytes 524312
  47.8 0.2 copy-done.1
  47.9 0.0 copy-start.2
  47.9 0.8 %copy-done.2 = bf16[16,16,1024]{2,1,0:T(8,128)(2,1)} copy-done((bf16[16,16,1024]{2,1,0:T(8,128)(2,1)}, bf16[16,16,1024]{2,1,0:T(8,128)(2,1)S(1)}, u32[]{:S(2)}) %copy-start.2) | copy-done | bytes 524312
  48.7 5.7 %cells.1 = f32[16,4,192]{2,1,0:T(4,128)} custom-call(bf16[36,128,256]{2,1,0:T(8,128)(2,1)} %denoise.1.denoised_ref, s32[16,64]{1,0:T(8,128)} %cell_ref.1, s32[16,64]{1,0:T(8,128)} %window_ref.1, bf16[16,16,1024]{2,1,0:T(8,128)(2,1)} %refs_0_.1, bf16[16,16,1024]{2,1,0:T(8,128)(2,1)} %copy-done, bf16[16,16,1024]{2,1,0:T(8,128)(2,1)} %copy-done.1, ...), custom_call_target="tpu_custom_call" | custom-call | flops 2147483648 | bytes 5242880 | tf_op jit(solution)/shard_map/cells/pallas_call | solution.py:504
  54.4 12.2 %all_to_all.5.moved_ref = f32[16,4,192]{2,1,0:T(4,128)} all-to-all(f32[16,4,192]{2,1,0:T(4,128)} %cells.1), channel_id=1, replica_groups=mesh['field'=2,'tm'=4,'tile'=4] {'tm','tile'}, dimensions={0} | all-to-all | bytes 98304 | tf_op jit(solution)/shard_map/all_to_all | solution.py:571
  66.6 1.5 %spikes.1 = f32[16,192]{1,0:T(8,128)} custom-call(f32[16,4,192]{2,1,0:T(4,128)} %all_to_all.5.moved_ref, f32[1,192]{1,0:T(1,128)} %bitcast.2), custom_call_target="tpu_custom_call" | custom-call | tf_op jit(solution)/shard_map/spikes/pallas_call | solution.py:572
Async XLA Ops:
  0.9 9.4 %collective-permute-start = (bf16[4,8,1024]{2,1,0:T(8,128)(2,1)S(1)}, bf16[4,8,1024]{2,1,0:T(8,128)(2,1)S(1)}, u32[]{:S(2)}, u32[]{:S(2)}) collective-permute-start(bf16[4,8,1024]{2,1,0:T(8,128)(2,1)S(1)} %get-tuple-element.6), channel_id=1, source_target_pairs={{0,1},{1,2},{2,3},{4,5},{5,6},{6,7},{8,9},{9,10},{10,11},{12,13},{... | collective-permute-start | bytes 196616 | tf_op jit(solution)/shard_map/ppermute | solution.py:554
  5.8 6.2 %collective-permute-start.1 = (bf16[4,8,1024]{2,1,0:T(8,128)(2,1)S(1)}, bf16[4,8,1024]{2,1,0:T(8,128)(2,1)S(1)}, u32[]{:S(2)}, u32[]{:S(2)}) collective-permute-start(bf16[4,8,1024]{2,1,0:T(8,128)(2,1)S(1)} %get-tuple-element.5), channel_id=1, source_target_pairs={{1,0},{2,1},{3,2},{5,4},{6,5},{7,6},{9,8},{10,9},{11,10},{13,12},{... | collective-permute-start | bytes 196616 | tf_op jit(solution)/shard_map/ppermute | solution.py:555
  7.1 39.8 %collective-permute-start.2 = (bf16[16,16,1024]{2,1,0:T(8,128)(2,1)}, bf16[16,16,1024]{2,1,0:T(8,128)(2,1)S(1)}, u32[]{:S(2)}, u32[]{:S(2)}) collective-permute-start(bf16[16,16,1024]{2,1,0:T(8,128)(2,1)} %refs_0_.1), channel_id=1, source_target_pairs={{0,12},{4,0},{8,4},{12,8},{1,13},{5,1},{9,5},{13,9},{2,14},{6,2},{... | collective-permute-start | bytes 1572872 | tf_op jit(solution)/shard_map/ppermute | solution.py:559
  7.9 39.1 %collective-permute-start.3 = (bf16[16,16,1024]{2,1,0:T(8,128)(2,1)}, bf16[16,16,1024]{2,1,0:T(8,128)(2,1)S(1)}, u32[]{:S(2)}, u32[]{:S(2)}) collective-permute-start(bf16[16,16,1024]{2,1,0:T(8,128)(2,1)} %refs_0_.1), channel_id=1, source_target_pairs={{0,8},{4,12},{8,0},{12,4},{1,9},{5,13},{9,1},{13,5},{2,10},{6,14},... | collective-permute-start | bytes 1572872 | tf_op jit(solution)/shard_map/ppermute | solution.py:559
  8.8 38.2 %collective-permute-start.4 = (bf16[16,16,1024]{2,1,0:T(8,128)(2,1)}, bf16[16,16,1024]{2,1,0:T(8,128)(2,1)S(1)}, u32[]{:S(2)}, u32[]{:S(2)}) collective-permute-start(bf16[16,16,1024]{2,1,0:T(8,128)(2,1)} %refs_0_.1), channel_id=1, source_target_pairs={{0,4},{4,8},{8,12},{12,0},{1,5},{5,9},{9,13},{13,1},{2,6},{6,10},{... | collective-permute-start | bytes 1572872 | tf_op jit(solution)/shard_map/ppermute | solution.py:559
  10.3 1.7 %copy-start.3 = (bf16[4,8,1024]{2,1,0:T(8,128)(2,1)}, bf16[4,8,1024]{2,1,0:T(8,128)(2,1)S(1)}, u32[]{:S(2)}) copy-start(bf16[4,8,1024]{2,1,0:T(8,128)(2,1)S(1)} %collective-permute-done.above_ref) | copy-start | bytes 196612
  12.0 0.6 copy-start.4
  47.0 0.8 %copy-start = (bf16[16,16,1024]{2,1,0:T(8,128)(2,1)}, bf16[16,16,1024]{2,1,0:T(8,128)(2,1)S(1)}, u32[]{:S(2)}) copy-start(bf16[16,16,1024]{2,1,0:T(8,128)(2,1)S(1)} %collective-permute-done.2.refs_1_) | copy-start | bytes 1572868
  47.0 1.0 %copy-start.1 = (bf16[16,16,1024]{2,1,0:T(8,128)(2,1)}, bf16[16,16,1024]{2,1,0:T(8,128)(2,1)S(1)}, u32[]{:S(2)}) copy-start(bf16[16,16,1024]{2,1,0:T(8,128)(2,1)S(1)} %collective-permute-done.3.refs_2_) | copy-start | bytes 1572868
  47.9 0.8 %copy-start.2 = (bf16[16,16,1024]{2,1,0:T(8,128)(2,1)}, bf16[16,16,1024]{2,1,0:T(8,128)(2,1)S(1)}, u32[]{:S(2)}) copy-start(bf16[16,16,1024]{2,1,0:T(8,128)(2,1)S(1)} %collective-permute-done.4.refs_3_) | copy-start | bytes 1572868
